TPU v7x, 512 devices: a whole 4x8x8 slice. The times are simulated.
512 devices in a mesh: stream: 32 (over x, z), span: 16 (over y, core).
Axes of the slice: x: 4, y: 8, z: 8, core: 2. Of those that a mesh axis runs over, the one named last changes fastest.
Arguments:
- rhs: float32 [32, 16, 2, 320, 128], P('stream', 'span'), may hold values from -6 to 6
- inv_blocks: bfloat16 [32, 16, 2, 320, 320], P('stream', 'span')
- coupling: bfloat16 [6, 320, 320], replicated, may hold values from -0.109375 to 0.109375
- trace_ops: bfloat16 [4, 80, 320], replicated, may hold values from -0.3125 to 0.3125
- lift_ops: bfloat16 [4, 320, 80], replicated
- order: int32 [32, 16, 2], P('stream', 'span'), may hold values from 0 to 1, each once within a row
- counts: int32 [32, 16], P('stream', 'span'), may hold values from 1 to 2, as said below
- neighbours: int32 [32, 16, 2, 2], P('stream', 'span'), may hold values from 0 to 2, as said below
- face_ids: int32 [32, 16, 2, 2], P('stream', 'span'), may hold values from 0 to 5
Outputs:
- solution: float32 [32, 16, 2, 320, 128], P('stream', 'span')
Inputs may be any that keep to these rules, and one draw needn't show every extreme that they name: order[i, j] lists each of the 2 slots of line (i, j) once. `counts`: some line holds 2 live elements and some line 1. `neighbours`: a slot of the same line other than the element's own, or 2 where the face has no in-line neighbour.
All inputs are finite; a program needn't handle non-finite values.
Results may differ from a plain program's by a relative error of at most 0.00075.
Values sent between devices are 32-bit elements; how exact they have to be, the bound alone decides.
A program may use at most 64 MiB of HBM per device.

v0:
```python
from functools import partial

import jax
import jax.numpy as jnp
from jax import lax
from jax.sharding import PartitionSpec as P

SWEEPS = 2


HIGH = lax.Precision.HIGHEST


def passed_along(block, axis, distance):
    devices = range(lax.axis_size(axis))
    route = [((i - distance) % len(devices), i) for i in devices]
    return lax.ppermute(block, axis, route)


def passed_along_2(block, axis, distance):
    devices = range(lax.axis_size(axis))
    route = [(i - distance, i) for i in devices if i - distance in devices]
    return lax.ppermute(block, axis, route)


def prefix(part, axis, combine, identity, reverse):
    count = lax.axis_size(axis)
    place = lax.axis_index(axis)
    ahead = count - 1 - place if reverse else place
    gathered = jax.tree.map(lambda a: lax.all_gather(a, axis), part)
    state = jax.tree.map(lambda a, e: jnp.zeros_like(a) + jnp.asarray(e, a.dtype), part, identity)

    def one(lap, state):
        source = count - 1 - lap if reverse else lap
        return combine(
            state, jax.tree.map(lambda a: lax.dynamic_index_in_dim(a, source, 0, False), gathered)
        )

    return lax.fori_loop(0, ahead, one, state)


def column_sweep(
    solution, residual, inverse, order, count, neighbours, face_ids, coupling, backward
):
    slot_count = solution.shape[0]
    positions = range(slot_count - 1, -1, -1) if backward else range(slot_count)
    for position in positions:
        slot_index = order[position]
        residual_now = lax.dynamic_index_in_dim(residual, slot_index, 0, keepdims=False)
        for face_index in range(neighbours.shape[1]):
            neighbour_slot = neighbours[slot_index, face_index]
            present = neighbour_slot < slot_count
            neighbour_block = lax.dynamic_index_in_dim(
                solution, jnp.minimum(neighbour_slot, slot_count - 1), 0, keepdims=False
            )
            coupling_block = lax.dynamic_index_in_dim(
                coupling, face_ids[slot_index, face_index], 0, keepdims=False
            )
            product = jnp.dot(coupling_block, neighbour_block, precision=HIGH)
            residual_now = residual_now - jnp.where(present, product, jnp.zeros_like(product))
        inverse_block = lax.dynamic_index_in_dim(inverse, slot_index, 0, keepdims=False).astype(
            jnp.float32
        )
        live_factor = (position < count).astype(jnp.float32)
        updated = jnp.dot(inverse_block, residual_now, precision=HIGH) * live_factor
        solution = lax.dynamic_update_index_in_dim(solution, updated, slot_index, 0)
    return solution


def apply_trace(operator, values):
    return jnp.einsum("tb,ebr->etr", operator, values, precision=HIGH)


def apply_lift(operator, traces):
    return jnp.einsum("bt,etr->ebr", operator, traces, precision=HIGH)


def compose(earlier, later):
    first_map, first_shift = earlier
    second_map, second_shift = later
    joined_map = jnp.dot(second_map, first_map, precision=HIGH)
    joined_shift = jnp.dot(second_map, first_shift, precision=HIGH) + second_shift
    return (joined_map, joined_shift)


def local(rhs, inv_blocks, coupling, trace_ops, lift_ops, order, counts, neighbours, face_ids):
    source = rhs[0, 0]
    inverse = inv_blocks[0, 0]
    sweep_order = order[0, 0]
    live_count = counts[0, 0]
    line_links = neighbours[0, 0]
    link_types = face_ids[0, 0]
    coupling_table = coupling.astype(jnp.float32)
    traces_op = trace_ops.astype(jnp.float32)
    lifts = lift_ops.astype(jnp.float32)
    slot_count, block_width, columns = source.shape
    face_width = traces_op.shape[1]
    state_width = slot_count * face_width
    line_sweep = partial(
        column_sweep,
        inverse=inverse,
        order=sweep_order,
        count=live_count,
        neighbours=line_links,
        face_ids=link_types,
        coupling=coupling_table,
    )
    selector = jnp.eye(slot_count, dtype=jnp.float32)

    def response(inflow_lift, outflow_trace, backward):
        entry_terms = -jnp.einsum("ef,bt->ebft", selector, inflow_lift, precision=HIGH).reshape(
            slot_count, block_width, state_width
        )
        response_field = line_sweep(jnp.zeros_like(entry_terms), entry_terms, backward=backward)
        transfer_map = apply_trace(outflow_trace, response_field).reshape(state_width, state_width)
        return (response_field, transfer_map)

    forward_maps = response(lifts[0], traces_op[1], False)
    backward_maps = response(lifts[1], traces_op[0], True)
    identity_pair = (
        jnp.eye(state_width, dtype=jnp.float32),
        jnp.zeros((state_width, columns), jnp.float32),
    )

    def half_sweep(solution, backward, first):
        residual_base = source
        if not first:
            from_left = passed_along(solution, "span", 1)
            from_right = passed_along(solution, "span", -1)
            left_traces = apply_trace(traces_op[3], from_left)
            right_traces = apply_trace(traces_op[2], from_right)
            residual_base = (
                residual_base
                - apply_lift(lifts[2], left_traces)
                - apply_lift(lifts[3], right_traces)
            )
            if backward:
                behind = passed_along_2(apply_trace(traces_op[1], solution), "stream", 1)
                residual_base = residual_base - apply_lift(lifts[0], behind)
            else:
                downstream = passed_along_2(apply_trace(traces_op[0], solution), "stream", -1)
                residual_base = residual_base - apply_lift(lifts[1], downstream)
        if backward:
            response_field, transfer_map = backward_maps
            outflow = traces_op[0]
        else:
            response_field, transfer_map = forward_maps
            outflow = traces_op[1]
        local_field = line_sweep(solution, residual_base, backward=backward)
        local_shift = apply_trace(outflow, local_field).reshape(state_width, columns)
        if backward:
            inflow_pair = prefix(
                (transfer_map, local_shift), "stream", compose, identity_pair, True
            )
        else:
            inflow_pair = prefix(
                (transfer_map, local_shift), "stream", compose, identity_pair, False
            )
        inflow = inflow_pair[1]
        return local_field + jnp.einsum("ebs,sr->ebr", response_field, inflow, precision=HIGH)

    solution = jnp.zeros_like(source)
    for sweep_index in range(SWEEPS):
        solution = half_sweep(solution, False, sweep_index == 0)
        solution = half_sweep(solution, True, False)
    return solution[None, None]


def solution(mesh):
    placed = (
        P("stream", "span", None, None, None),
        P("stream", "span", None, None, None),
        P(),
        P(),
        P(),
        P("stream", "span", None),
        P("stream", "span"),
        P("stream", "span", None, None),
        P("stream", "span", None, None),
    )
    return jax.shard_map(
        local,
        mesh=mesh,
        in_specs=placed,
        out_specs=P("stream", "span", None, None, None),
        check_vma=False,
    )
```

profile of v0, /device:TPU:8, one launch (start us, length us, event | category | flops | bytes accessed | tf_op | source)
XLA Modules:
  0.0 704.1 jit_solution(7536998837973001585)
XLA Ops:
  6.5 1.4 fusion.278
  11.8 1.5 constant_dynamic-slice_fusion
  25.6 1.3 fusion.39
  36.9 1.4 fusion.29
  40.4 78.8 %all-gather.9.cloned.1.call-done = f32[32,160,128]{2,1,0:T(8,128)} async-done(((f32[1,160,128]{2,1,0:T(8,128)}), f32[32,160,128]{2,1,0:T(8,128)}) %all-gather.9.cloned.1.call-update) | async-done | bytes 2621456 | tf_op jit(solution)/shard_map/all_gather | solution.py:30
  119.2 90.6 %all-gather.7.cloned.1.call-done = f32[32,160,160]{2,1,0:T(8,128)} async-done(((f32[1,160,160]{2,1,0:T(8,128)}), f32[32,160,160]{2,1,0:T(8,128)}) %all-gather.7.cloned.1.call-update) | async-done | bytes 3276816 | tf_op jit(solution)/shard_map/all_gather | solution.py:30
  209.8 2.4 convolution_add_fusion.7
  212.2 1.7 collective-permute-start.1
  215.0 5.0 collective-permute-start.2
  225.0 75.5 %all-gather.11.cloned.1.call-done = f32[32,160,160]{2,1,0:T(8,128)} async-done(((f32[1,160,160]{2,1,0:T(8,128)}), f32[32,160,160]{2,1,0:T(8,128)}) %all-gather.11.cloned.1.call-update) | async-done | bytes 3276816 | tf_op jit(solution)/shard_map/all_gather | solution.py:30
  300.4 84.4 %all-gather.13.cloned.1.call-done = f32[32,160,128]{2,1,0:T(8,128)} async-done(((f32[1,160,128]{2,1,0:T(8,128)}), f32[32,160,128]{2,1,0:T(8,128)}) %all-gather.13.cloned.1.call-update) | async-done | bytes 2621456 | tf_op jit(solution)/shard_map/all_gather | solution.py:30
  384.8 40.4 %while.53 = (s32[]{:T(128)}, f32[160,128]{1,0:T(8,128)S(1)}, s32[]{:T(128)}, f32[32,160,160]{2,1,0:T(8,128)}, f32[32,160,128]{2,1,0:T(8,128)}, /*index=5*/s32[]{:T(128)}, s32[]{:T(128)}, s32[]{:T(128)}, s32[]{:T(128)}) while((s32[]{:T(128)}, f32[160,128]{1,0:T(8,128)S(1)}, s32[]{:T(128)}, f32[32,160,160]{2,1,0:T(8,128)}, ...), condition=%wide.region_3.4_spmd, body=%wide.region_2.3_spmd.sunk | while | flops 39342084 | bytes 574603 | solution.py:39
  425.3 1.3 convolution_add_fusion.6
  426.6 1.7 collective-permute-start.4
  429.5 1.3 collective-permute-start.5
  431.1 2.0 collective-permute-done.3
  434.4 1.4 collective-permute-done.5
  439.6 79.2 %all-gather.15.cloned.1.call-done = f32[32,160,128]{2,1,0:T(8,128)} async-done(((f32[1,160,128]{2,1,0:T(8,128)}), f32[32,160,128]{2,1,0:T(8,128)}) %all-gather.15.cloned.1.call-update) | async-done | bytes 2621456 | tf_op jit(solution)/shard_map/all_gather | solution.py:30
  518.8 2.4 convolution_add_fusion.5
  521.2 1.7 collective-permute-start.7
  524.0 4.1 collective-permute-start.8
  533.0 121.9 %all-gather.17.cloned.1.call-done = f32[32,160,128]{2,1,0:T(8,128)} async-done(((f32[1,160,128]{2,1,0:T(8,128)}), f32[32,160,128]{2,1,0:T(8,128)}) %all-gather.17.cloned.1.call-update) | async-done | bytes 2621456 | tf_op jit(solution)/shard_map/all_gather | solution.py:30
  654.8 40.3 %while.55 = (s32[]{:T(128)}, f32[160,128]{1,0:T(8,128)S(1)}, s32[]{:T(128)}, f32[32,160,160]{2,1,0:T(8,128)}, f32[32,160,128]{2,1,0:T(8,128)}, /*index=5*/s32[]{:T(128)}, s32[]{:T(128)}, s32[]{:T(128)}, s32[]{:T(128)}) while((s32[]{:T(128)}, f32[160,128]{1,0:T(8,128)S(1)}, s32[]{:T(128)}, f32[32,160,160]{2,1,0:T(8,128)}, ...), condition=%wide.region_7.8_spmd, body=%wide.region_6.7_spmd.sunk | while | flops 39342084 | bytes 574603 | solution.py:39
  695.2 2.0 fusion.12
  (250 shorter events, 107.6 us)
Async XLA Ops:
  6.5 18.7 %copy-start = (bf16[6,320,320]{2,1,0:T(8,128)(2,1)S(1)}, bf16[6,320,320]{2,1,0:T(8,128)(2,1)}, u32[]{:S(2)}) copy-start(bf16[6,320,320]{2,1,0:T(8,128)(2,1)} %param.19) | copy-start | bytes 3686404
  6.5 20.7 %copy-start.3 = (f32[1,1,2,320,128]{4,3,2,1,0:T(8,128)S(1)}, f32[1,1,2,320,128]{4,3,2,1,0:T(8,128)}, u32[]{:S(2)}) copy-start(f32[1,1,2,320,128]{4,3,2,1,0:T(8,128)} %param.17) | copy-start | bytes 983044
  6.5 20.4 %copy-start.1 = (bf16[1,1,2,320,320]{4,3,2,1,0:T(8,128)(2,1)S(1)}, bf16[1,1,2,320,320]{4,3,2,1,0:T(8,128)(2,1)}, u32[]{:S(2)}) copy-start(bf16[1,1,2,320,320]{4,3,2,1,0:T(8,128)(2,1)} %param.18) | copy-start | bytes 1228804
  6.5 112.7 %all-gather.9.cloned.1.call-start = ((), (), s32[]{:S(2)}) async-start(), calls=%async_computation.1 | async-start | bytes 2703360 | tf_op jit(solution)/shard_map/all_gather | solution.py:30
  30.0 179.8 %all-gather.7.cloned.1.call-start = ((), (), s32[]{:S(2)}) async-start(), calls=%async_computation | async-start | bytes 5406720 | tf_op jit(solution)/shard_map/all_gather | solution.py:30
  34.2 266.3 %all-gather.11.cloned.1.call-start = ((), (), s32[]{:S(2)}) async-start(), calls=%async_computation.2 | async-start | bytes 5406720 | tf_op jit(solution)/shard_map/all_gather | solution.py:30
  40.4 344.5 %all-gather.13.cloned.1.call-start = ((), (), s32[]{:S(2)}) async-start(), calls=%async_computation.3 | async-start | bytes 2703360 | tf_op jit(solution)/shard_map/all_gather | solution.py:30
  209.8 10.6 %copy-start.9 = (bf16[4,80,320]{2,1,0:T(8,128)(2,1)S(1)}, bf16[4,80,320]{2,1,0:T(8,128)(2,1)}, u32[]{:S(2)}) copy-start(bf16[4,80,320]{2,1,0:T(8,128)(2,1)} %param.20) | copy-start | bytes 614404
  209.8 11.1 %copy-start.4 = (f32[1,1,2,320,128]{4,3,2,1,0:T(8,128)S(1)}, f32[1,1,2,320,128]{4,3,2,1,0:T(8,128)}, u32[]{:S(2)}) copy-start(f32[1,1,2,320,128]{4,3,2,1,0:T(8,128)} %param.17) | copy-start | bytes 983044
  209.8 11.1 %copy-start.14 = (bf16[4,320,80]{1,2,0:T(8,128)(2,1)S(1)}, bf16[4,320,80]{1,2,0:T(8,128)(2,1)}, u32[]{:S(2)}) copy-start(bf16[4,320,80]{1,2,0:T(8,128)(2,1)} %param.21) | copy-start | bytes 614404
  212.2 8.2 %collective-permute-start = (f32[2,320,128]{2,1,0:T(8,128)S(1)}, f32[2,320,128]{2,1,0:T(8,128)S(1)}, u32[]{:S(2)}, u32[]{:S(2)}) collective-permute-start(f32[2,320,128]{2,1,0:T(8,128)S(1)} %convolution_add_fusion.7), channel_id=1, source_target_pairs={{15,0},{0,1},{1,2},{2,3},{3,4},{4,5},{5,6},{6,7},{7,8},{8,9},{9,10... | collective-permute-start | bytes 983048 | tf_op jit(solution)/shard_map/ppermute | solution.py:17
  212.2 8.5 %collective-permute-start.1 = (f32[2,320,128]{2,1,0:T(8,128)S(1)}, f32[2,320,128]{2,1,0:T(8,128)S(1)}, u32[]{:S(2)}, u32[]{:S(2)}) collective-permute-start(f32[2,320,128]{2,1,0:T(8,128)S(1)} %convolution_add_fusion.7), channel_id=1, source_target_pairs={{1,0},{2,1},{3,2},{4,3},{5,4},{6,5},{7,6},{8,7},{9,8},{10,9},{11,1... | collective-permute-start | bytes 983048 | tf_op jit(solution)/shard_map/ppermute | solution.py:17
  215.0 6.9 collective-permute-start.2
  224.9 293.9 %all-gather.15.cloned.1.call-start = ((), (), s32[]{:S(2)}) async-start(), calls=%async_computation.4 | async-start | bytes 2703360 | tf_op jit(solution)/shard_map/all_gather | solution.py:30
  426.6 6.5 collective-permute-start.3
  426.6 7.1 %collective-permute-start.4 = (f32[2,320,128]{2,1,0:T(8,128)S(1)}, f32[2,320,128]{2,1,0:T(8,128)S(1)}, u32[]{:S(2)}, u32[]{:S(2)}) collective-permute-start(f32[2,320,128]{2,1,0:T(8,128)S(1)} %convolution_add_fusion.6), channel_id=1, source_target_pairs={{1,0},{2,1},{3,2},{4,3},{5,4},{6,5},{7,6},{8,7},{9,8},{10,9},{11,1... | collective-permute-start | bytes 983048 | tf_op jit(solution)/shard_map/ppermute | solution.py:17
  429.5 6.3 collective-permute-start.5
  439.6 215.3 %all-gather.17.cloned.1.call-start = ((), (), s32[]{:S(2)}) async-start(), calls=%async_computation.5 | async-start | bytes 2703360 | tf_op jit(solution)/shard_map/all_gather | solution.py:30
  518.8 9.7 %copy-start.11 = (bf16[4,80,320]{2,1,0:T(8,128)(2,1)S(1)}, bf16[4,80,320]{2,1,0:T(8,128)(2,1)}, u32[]{:S(2)}) copy-start(bf16[4,80,320]{2,1,0:T(8,128)(2,1)} %param.20) | copy-start | bytes 614404
  518.8 10.0 %copy-start.6 = (f32[1,1,2,320,128]{4,3,2,1,0:T(8,128)S(1)}, f32[1,1,2,320,128]{4,3,2,1,0:T(8,128)}, u32[]{:S(2)}) copy-start(f32[1,1,2,320,128]{4,3,2,1,0:T(8,128)} %param.17) | copy-start | bytes 983044
  518.8 10.0 %copy-start.16 = (bf16[4,320,80]{1,2,0:T(8,128)(2,1)S(1)}, bf16[4,320,80]{1,2,0:T(8,128)(2,1)}, u32[]{:S(2)}) copy-start(bf16[4,320,80]{1,2,0:T(8,128)(2,1)} %param.21) | copy-start | bytes 614404
  521.2 7.3 %collective-permute-start.6 = (f32[2,320,128]{2,1,0:T(8,128)S(1)}, f32[2,320,128]{2,1,0:T(8,128)S(1)}, u32[]{:S(2)}, u32[]{:S(2)}) collective-permute-start(f32[2,320,128]{2,1,0:T(8,128)S(1)} %convolution_add_fusion.5), channel_id=1, source_target_pairs={{15,0},{0,1},{1,2},{2,3},{3,4},{4,5},{5,6},{6,7},{7,8},{8,9},{9,10... | collective-permute-start | bytes 983048 | tf_op jit(solution)/shard_map/ppermute | solution.py:17
  521.2 7.9 %collective-permute-start.7 = (f32[2,320,128]{2,1,0:T(8,128)S(1)}, f32[2,320,128]{2,1,0:T(8,128)S(1)}, u32[]{:S(2)}, u32[]{:S(2)}) collective-permute-start(f32[2,320,128]{2,1,0:T(8,128)S(1)} %convolution_add_fusion.5), channel_id=1, source_target_pairs={{1,0},{2,1},{3,2},{4,3},{5,4},{6,5},{7,6},{8,7},{9,8},{10,9},{11,1... | collective-permute-start | bytes 983048 | tf_op jit(solution)/shard_map/ppermute | solution.py:17
  524.0 5.9 collective-permute-start.8
  (8 other events, 36.3 us)
Sparse Core Ops, SparseCore 0:
  30.1 89.0 all-gather.8
  122.4 87.3 all-gather.6
  213.0 87.4 all-gather.10
  303.5 81.3 all-gather.12
  439.7 79.0 all-gather.14
  533.1 121.6 all-gather.16
where the time goes:
time: 706 us; the launch traced here: 704 us
  waiting for transfers between devices  534 us (76%)
  matrix products  115 us (16%)
  between operations  31.3 us (4%)
  starting transfers between devices  15.8 us (2%)
    all_gather x6, waiting for transfers between devices, prefix(): gathered = jax.tree.map(lambda a: lax.all_gather(a, axis), part)  530 us
    dot_general x62, matrix products, compose(): jnp.dot(second_map, first_shift, precision=HIGH) + second_shift  77.9 us
  transfers between devices with their start and end apart: 15, of which 10 were waited for; matrix products, arithmetic and copies ran while one was open for 3% of the time, Pallas kernels for 0%

commit v1 on v0

v1 whole, which is shorter than its diff:
```python
import functools

import jax
import jax.numpy as jnp
from jax import lax
from jax.experimental import pallas as pl
from jax.experimental.pallas import tpu as pltpu
from jax.sharding import PartitionSpec as P

MESH = pl.DeviceIdType.MESH
F32 = jnp.float32
BF16 = jnp.bfloat16
SWEEPS = 2
B = 320
TF = 80
W = 128


def split(v):
    high = v.astype(BF16)
    return high, (v - high.astype(F32)).astype(BF16)


def apply(operator, v):
    high, low = split(v)
    both = jnp.dot(operator, jnp.concatenate([high, low], axis=1), preferred_element_type=F32)
    return both[:, :W] + both[:, W:]


def nt(a, b):
    return lax.dot_general(a, b, (((1,), (1,)), ((), ())), preferred_element_type=F32)


def through(v, high_map, low_map):
    high, low = split(v)
    rows = v.shape[0]
    both = nt(jnp.concatenate([high, low], axis=0), high_map)
    return both[:rows] + both[rows:] + nt(high, low_map)


def kernel(
    NX, NZ, NS,
    order_ref, count_ref, nbr_ref, fid_ref, rhs_ref, inv_ref, coup_ref, trop_ref, lift_ref,
    out_ref,
    invs, coups, lpad, tpad, base, resid, field,
    tmsg, tmap, cmap, sstage, sbuf, lbuf, ostage, wbuf, xstage, xbuf, icur, pstage, pbuf,
    tsend, trecv, asend, arecv, bsend, brecv, xsend, xrecv, psend, precv,
):
    CH = W // NZ
    i = lax.axis_index("stream")
    j = lax.axis_index("span")
    z = lax.rem(i, NZ)
    x = lax.div(i, NZ)

    def at_z(offset):
        return lax.rem(z + (offset + NZ), NZ)

    def line_z(zz):
        return (x * NZ + zz, j)

    span_left = (i, lax.rem(j + NS - 1, NS))
    span_right = (i, lax.rem(j + 1, NS))
    x_next = (lax.rem(x + 1, NX) * NZ + z, j)
    x_prev = (lax.rem(x + NX - 1, NX) * NZ + z, j)

    barrier = pltpu.get_barrier_semaphore()
    greeted = [line_z(at_z(d)) for d in range(1, NZ)] + [x_next, x_prev, span_left, span_right]
    for device in greeted:
        pl.semaphore_signal(barrier, inc=1, device_id=device, device_id_type=MESH)

    a = order_ref[0, 0, 0]
    b = order_ref[0, 0, 1]
    a_is_0 = a == 0
    live = count_ref[0, 0] > 1
    zero_block = jnp.zeros((B, B), BF16)
    invs[0] = inv_ref[a]
    invs[1] = jnp.where(live, inv_ref[b], zero_block)
    for pos, slot in ((0, a), (1, b)):
        for m in range(2):
            present = nbr_ref[0, 0, slot, m] < 2
            coups[pos, m] = jnp.where(present, coup_ref[fid_ref[0, 0, slot, m]], zero_block)
        base[pos] = rhs_ref[slot]
        resid[pos] = rhs_ref[slot]
        field[pos] = jnp.zeros((B, W), F32)
    lpad[...] = jnp.zeros((2, B, W), BF16)
    tpad[...] = jnp.zeros((2, W, B), BF16)
    for d in range(2):
        lpad[d, :, 0:TF] = lift_ref[d]
        tpad[d, 0:TF, :] = trop_ref[1 - d]
    tmap[...] = jnp.zeros(tmap.shape, BF16)

    def coupled(pos, v):
        high, low = split(v)
        v2 = jnp.concatenate([high, low], axis=1)
        both = jnp.dot(coups[pos, 0], v2, preferred_element_type=F32) + jnp.dot(
            coups[pos, 1], v2, preferred_element_type=F32
        )
        return both[:, :W] + both[:, W:]

    lane = lax.broadcasted_iota(jnp.int32, (TF, W), 1)

    def own_map(d):
        first, second = (0, 1) if d == 0 else (1, 0)
        u1 = jnp.dot(invs[first], lpad[d], preferred_element_type=F32)
        u2 = jnp.dot(invs[second], lpad[d], preferred_element_type=F32)
        v = apply(invs[second], coupled(second, u1))
        trace = trop_ref[1 - d]
        t11 = -apply(trace, u1)
        t22 = -apply(trace, u2)
        t21 = apply(trace, v)
        first_is_0 = jnp.where(a_is_0, 1.0 - d, 0.0 + d).astype(F32)
        flag = jnp.zeros((TF, W), F32) + first_is_0
        upper = jnp.where(lane < TF, t11, jnp.where(lane < 112, pltpu.roll(t22, 32, 1), flag))
        lower = jnp.where(lane < TF, t21, pltpu.roll(t22, TF, 1))
        tmsg[d, z, 0:TF, :] = upper
        tmsg[d, z, TF : 2 * TF, :] = lower

    def unpack(d, zz):
        p = zz if d == 0 else NZ - 1 - zz
        upper = tmsg[d, zz, 0:TF, :]
        lower = tmsg[d, zz, TF : 2 * TF, :]
        flag = jnp.sum(jnp.where(lane == 120, upper, 0.0), axis=1, keepdims=True) > 0.5
        zero = jnp.zeros((TF, W), F32)
        t11 = jnp.where(lane < TF, upper, zero)
        t21 = jnp.where(lane < TF, lower, zero)
        t22 = jnp.where(
            lane < 48,
            pltpu.roll(lower, 48, 1),
            jnp.where(lane < TF, pltpu.roll(upper, 96, 1), zero),
        )
        blocks = (
            (0, 0, jnp.where(flag, t11, t22)),
            (0, W, jnp.where(flag, zero, t21)),
            (W, 0, jnp.where(flag, t21, zero)),
            (W, W, jnp.where(flag, t22, t11)),
        )
        for row, col, block in blocks:
            high, low = split(block)
            tmap[d, p, 0, row : row + TF, col : col + W] = high
            tmap[d, p, 1, row : row + TF, col : col + W] = low

    def t_copy(d, ring, k, zz):
        step = 1 if ring == 0 else -1
        return pltpu.make_async_remote_copy(
            src_ref=tmsg.at[d, zz],
            dst_ref=tmsg.at[d, zz],
            send_sem=tsend.at[d, ring, k],
            recv_sem=trecv.at[d, ring, k],
            device_id=line_z(at_z(step)),
            device_id_type=MESH,
        )

    reach = (NZ // 2, NZ - 1 - NZ // 2)
    for d in range(2):
        own_map(d)
        if d == 0:
            pl.semaphore_wait(barrier, len(greeted))
        for ring in range(2):
            if reach[ring] > 0:
                t_copy(d, ring, 0, z).start()
    for d in range(2):
        unpack(d, z)
    for k in range(1, NZ // 2 + 1):
        for d in range(2):
            for ring in range(2):
                if k > reach[ring]:
                    continue
                source = at_z(-k if ring == 0 else k)
                t_copy(d, ring, k - 1, source).wait_recv()
                if k < reach[ring]:
                    t_copy(d, ring, k, source).start()
            for ring in range(2):
                if k <= reach[ring]:
                    unpack(d, at_z(-k if ring == 0 else k))
    for d in range(2):
        for ring in range(2):
            for k in range(reach[ring]):
                t_copy(d, ring, k, at_z(-k if ring == 0 else k)).wait_send()

    for d in range(2):
        row = lax.broadcasted_iota(jnp.int32, (2 * W, 2 * W), 0)
        col = lax.broadcasted_iota(jnp.int32, (2 * W, 2 * W), 1)
        cmap[d, 0, 0] = jnp.where(row == col, 1.0, 0.0).astype(BF16)
        cmap[d, 0, 1] = jnp.zeros((2 * W, 2 * W), BF16)
        cmap[d, 1] = tmap[d, 0]

        def cumulate(p, carry, d=d):
            high, low = cmap[d, p, 0], cmap[d, p, 1]
            joined = (
                jnp.dot(tmap[d, p, 0], high, preferred_element_type=F32)
                + jnp.dot(tmap[d, p, 0], low, preferred_element_type=F32)
                + jnp.dot(tmap[d, p, 1], high, preferred_element_type=F32)
            )
            high, low = split(joined)
            cmap[d, p + 1, 0] = high
            cmap[d, p + 1, 1] = low
            return carry

        lax.fori_loop(1, NZ, cumulate, 0)

    far_first = sorted(range(1, NZ), key=lambda d: (-min(d, NZ - d), d))

    def a_copy(h, d):
        zz = at_z(d)
        return pltpu.make_async_remote_copy(
            src_ref=sstage.at[h, pl.ds(pl.multiple_of(zz * CH, CH), CH), :],
            dst_ref=sbuf.at[h, z],
            send_sem=asend.at[h, d],
            recv_sem=arecv.at[h, d],
            device_id=line_z(zz),
            device_id_type=MESH,
        )

    def b_copy(h, d):
        return pltpu.make_async_remote_copy(
            src_ref=ostage.at[h, d],
            dst_ref=wbuf.at[h, pl.ds(pl.multiple_of(z * CH, CH), CH), :],
            send_sem=bsend.at[h, d],
            recv_sem=brecv.at[h, d],
            device_id=line_z(at_z(d)),
            device_id_type=MESH,
        )

    def x_copy(h, device):
        return pltpu.make_async_remote_copy(
            src_ref=xstage.at[h],
            dst_ref=xbuf.at[h],
            send_sem=xsend.at[h],
            recv_sem=xrecv.at[h],
            device_id=device,
            device_id_type=MESH,
        )

    def p_copy(h, side, device):
        return pltpu.make_async_remote_copy(
            src_ref=pstage.at[h, side],
            dst_ref=pbuf.at[h, side],
            send_sem=psend.at[h, side],
            recv_sem=precv.at[h, side],
            device_id=device,
            device_id_type=MESH,
        )

    def half_sweep(k, d):
        h = 2 * k + d
        first, second = (0, 1) if d == 0 else (1, 0)
        x1 = apply(invs[first], resid[first] - coupled(first, field[second]))
        x2 = apply(invs[second], resid[second] - coupled(second, x1))
        s1 = apply(tpad[d], x1)
        s2 = apply(tpad[d], x2)
        sa, sb = (s1, s2) if d == 0 else (s2, s1)
        sstage[h, :, 0:W] = jnp.where(a_is_0, sa, sb).T
        sstage[h, :, W : 2 * W] = jnp.where(a_is_0, sb, sa).T
        for dist in far_first:
            a_copy(h, dist).start()
        sbuf[h, z] = sstage[h, pl.ds(pl.multiple_of(z * CH, CH), CH), :]
        for dist in far_first:
            a_copy(h, dist).wait_recv()

        v = jnp.zeros((CH, 2 * W), F32)
        for p in range(NZ):
            lbuf[p] = v
            new = sbuf[h, p if d == 0 else NZ - 1 - p]
            v = new if p == 0 else through(v, tmap[d, p, 0], tmap[d, p, 1]) + new

        xp = x if d == 0 else NX - 1 - x
        ahead, behind = (x_next, x_prev) if d == 0 else (x_prev, x_next)

        @pl.when(xp == 0)
        def _():
            icur[...] = jnp.zeros((CH, 2 * W), F32)

        @pl.when(xp > 0)
        def _():
            x_copy(h, behind).wait_recv()
            icur[...] = xbuf[h]

        inflow = icur[...]

        @pl.when(xp < NX - 1)
        def _():
            xstage[h] = v + through(inflow, cmap[d, NZ, 0], cmap[d, NZ, 1])
            x_copy(h, ahead).start()

        for dist in far_first + [0]:
            zz = at_z(dist)
            p = zz if d == 0 else NZ - 1 - zz
            piece = lbuf[p] + through(inflow, cmap[d, p, 0], cmap[d, p, 1])
            if dist:
                ostage[h, dist] = piece
                b_copy(h, dist).start()
            else:
                wbuf[h, pl.ds(pl.multiple_of(z * CH, CH), CH), :] = piece
        for dist in far_first:
            b_copy(h, dist).wait_recv()

        w0 = wbuf[h, :, 0:W].T[0:TF]
        w1 = wbuf[h, :, W : 2 * W].T[0:TF]
        wa = jnp.where(a_is_0, w0, w1)
        wb = jnp.where(a_is_0, w1, w0)
        lifted = (apply(lift_ref[d], wa), apply(lift_ref[d], wb))
        y1 = apply(invs[first], lifted[first])
        y2 = apply(invs[second], lifted[second] - coupled(second, y1))
        x1 = x1 - y1
        x2 = x2 - y2
        field[first] = x1
        field[second] = x2

        def exchange():
            xa, xb = (x1, x2) if d == 0 else (x2, x1)
            for side, trace, device in ((0, 3, span_right), (1, 2, span_left)):
                ta = apply(trop_ref[trace], xa)
                tb = apply(trop_ref[trace], xb)
                pstage[h, side, 0] = jnp.where(a_is_0, ta, tb)
                pstage[h, side, 1] = jnp.where(a_is_0, tb, ta)
                p_copy(h, side, device).start()
            rest = [base[pos] - lifted[pos] for pos in range(2)]
            p_copy(h, 0, span_right).wait_recv()
            p_copy(h, 1, span_left).wait_recv()
            for pos in range(2):
                total = rest[pos]
                for side in range(2):
                    t0 = pbuf[h, side, 0]
                    t1 = pbuf[h, side, 1]
                    mine, other = (t0, t1) if pos == 0 else (t1, t0)
                    total = total - apply(lift_ref[2 + side], jnp.where(a_is_0, mine, other))
                resid[pos] = total
            p_copy(h, 0, span_right).wait_send()
            p_copy(h, 1, span_left).wait_send()

        if d == 0:
            exchange()
        else:
            pl.when(k < SWEEPS - 1)(exchange)

        for dist in far_first:
            a_copy(h, dist).wait_send()
            b_copy(h, dist).wait_send()

        @pl.when(xp < NX - 1)
        def _():
            x_copy(h, ahead).wait_send()

    def sweep(k, carry):
        half_sweep(k, 0)
        half_sweep(k, 1)
        return carry

    lax.fori_loop(0, SWEEPS, sweep, 0)
    out_ref[0] = jnp.where(a_is_0, field[0], field[1])
    out_ref[1] = jnp.where(a_is_0, field[1], field[0])


def solution(mesh):
    lines = mesh.shape["stream"]
    NZ = {32: 8, 8: 4, 4: 2}[lines]
    NX = lines // NZ
    NS = mesh.shape["span"]
    CH = W // NZ
    H = 2 * SWEEPS

    def local(rhs, inv_blocks, coupling, trace_ops, lift_ops, order, counts, neighbours, face_ids):
        vmem = pl.BlockSpec(memory_space=pltpu.VMEM)
        smem = pl.BlockSpec(memory_space=pltpu.SMEM)
        dma = pltpu.SemaphoreType.DMA
        call = pl.pallas_call(
            functools.partial(kernel, NX, NZ, NS),
            out_shape=jax.ShapeDtypeStruct((2, B, W), F32),
            in_specs=[smem] * 4 + [vmem] * 5,
            out_specs=vmem,
            scratch_shapes=[
                pltpu.VMEM((2, B, B), BF16),
                pltpu.VMEM((2, 2, B, B), BF16),
                pltpu.VMEM((2, B, W), BF16),
                pltpu.VMEM((2, W, B), BF16),
                pltpu.VMEM((2, B, W), F32),
                pltpu.VMEM((2, B, W), F32),
                pltpu.VMEM((2, B, W), F32),
                pltpu.VMEM((2, NZ, 2 * TF, W), F32),
                pltpu.VMEM((2, NZ, 2, 2 * W, 2 * W), BF16),
                pltpu.VMEM((2, NZ + 1, 2, 2 * W, 2 * W), BF16),
                pltpu.VMEM((H, W, 2 * W), F32),
                pltpu.VMEM((H, NZ, CH, 2 * W), F32),
                pltpu.VMEM((NZ, CH, 2 * W), F32),
                pltpu.VMEM((H, NZ, CH, 2 * W), F32),
                pltpu.VMEM((H, W, 2 * W), F32),
                pltpu.VMEM((H, CH, 2 * W), F32),
                pltpu.VMEM((H, CH, 2 * W), F32),
                pltpu.VMEM((CH, 2 * W), F32),
                pltpu.VMEM((H, 2, 2, TF, W), F32),
                pltpu.VMEM((H, 2, 2, TF, W), F32),
                dma((2, 2, NZ)), dma((2, 2, NZ)),
                dma((H, NZ)), dma((H, NZ)),
                dma((H, NZ)), dma((H, NZ)),
                dma((H,)), dma((H,)),
                dma((H, 2)), dma((H, 2)),
            ],
            compiler_params=pltpu.CompilerParams(
                collective_id=0, has_side_effects=True, vmem_limit_bytes=48 << 20
            ),
        )
        result = call(
            order, counts, neighbours, face_ids,
            rhs[0, 0], inv_blocks[0, 0], coupling, trace_ops, lift_ops,
        )
        return result[None, None]

    placed = (
        P("stream", "span", None, None, None),
        P("stream", "span", None, None, None),
        P(),
        P(),
        P(),
        P("stream", "span", None),
        P("stream", "span"),
        P("stream", "span", None, None),
        P("stream", "span", None, None),
    )
    return jax.shard_map(
        local,
        mesh=mesh,
        in_specs=placed,
        out_specs=P("stream", "span", None, None, None),
        check_vma=False,
    )
```

time: 706 us -> 148 us (0.21)
  the two profiles are of different devices: /device:TPU:8 before, /device:TPU:48 now
where the time goes in v1:
time: 148 us
  Pallas kernels  139 us (94%)
  local copies, waits for them, and re-layouts  8.21 us (6%)
    pallas_call x1, Pallas kernels, local(): call(order, counts, neighbours, face_ids, rhs[0, 0], inv_blocks[0, 0], co...  139 us
    unnamed x16, local copies, waits for them, and re-layouts  8.21 us

profile of v1, /device:TPU:48, one launch (start us, length us, event | category | flops | bytes accessed | tf_op | source)
XLA Modules:
  0.0 148.0 jit_solution(10294534877977276313)
XLA Ops:
  0.7 1.2 copy.10.lift_ref
  1.8 0.0 copy-start
  1.8 1.4 copy-done
  3.2 0.0 copy-start.1
  3.2 1.0 copy-done.1
  4.2 0.0 copy-start.2
  4.2 1.0 copy-done.2
  5.2 0.0 copy-start.3
  5.2 0.9 copy-done.3
  6.1 0.0 copy-start.4
  6.1 0.7 copy-done.4
  6.8 0.0 copy-start.5
  6.8 0.7 copy-done.5
  7.5 0.0 copy-start.6
  7.5 0.7 copy-done.6
  8.2 139.1 %shard_map.91 = f32[2,320,128]{2,1,0:T(8,128)S(1)} custom-call(s32[1,1,2]{2,1,0:T(1,128)S(1)} %copy-done.6, s32[1,1]{1,0:T(1,128)S(6)} %copy.12.count_ref, s32[1,1,2,2]{3,2,1,0:T(2,128)S(1)} %copy-done.4, s32[1,1,2,2]{3,2,1,0:T(2,128)S(1)} %copy-done.5, f32[2,320,128]{2,1,0:T(8,128)S(1)} %bitcast.5, bf16[2,320,320]{2,1,0:T(8,128)(2,1)S(1)} %bitcast.4, ...), custom_call_target="tpu_custom_call" | custom-call | tf_op jit(solution)/shard_map/pallas_call | solution.py:402
  147.2 0.7 copy.13
Async XLA Ops:
  1.8 1.4 copy-start
  3.2 1.0 copy-start.1
  4.2 1.0 copy-start.2
  5.2 0.9 copy-start.3
  6.1 0.7 copy-start.4
  6.8 0.7 copy-start.5
  7.5 0.7 copy-start.6

commit v2 on v1

v2 whole, which is shorter than its diff:
```python
import functools

import jax
import jax.numpy as jnp
from jax import lax
from jax.experimental import pallas as pl
from jax.experimental.pallas import tpu as pltpu
from jax.sharding import PartitionSpec as P

MESH = pl.DeviceIdType.MESH
F32 = jnp.float32
BF16 = jnp.bfloat16
SWEEPS = 2
B = 320
TF = 80
W = 128


def split(v):
    high = v.astype(BF16)
    return high, (v - high.astype(F32)).astype(BF16)


def apply(operator, v):
    high, low = split(v)
    both = jnp.dot(operator, jnp.concatenate([high, low], axis=1), preferred_element_type=F32)
    return both[:, :W] + both[:, W:]


def nt(a, b):
    return lax.dot_general(a, b, (((1,), (1,)), ((), ())), preferred_element_type=F32)


def through(v, high_map, low_map):
    high, low = split(v)
    rows = v.shape[0]
    both = nt(jnp.concatenate([high, low], axis=0), high_map)
    return both[:rows] + both[rows:] + nt(high, low_map)


def kernel(
    NX, NZ, NS,
    order_hbm, count_hbm, nbr_hbm, fid_hbm, rhs_hbm, inv_hbm, coup_hbm, trop_hbm, liftt_hbm,
    out_ref,
    order_ref, count_ref, nbr_ref, fid_ref, rhs_ref, inv_ref, coup_ref, trop_ref, liftt_ref,
    invs, coups, lpad, ltpad, tpad, base, resid, field,
    tmsg, tmap, prod, dmap, dmsg, dbuf, sstage, sbuf, ostage, wbuf, gstage, gbuf, icur, pstage, pbuf,
    insem, tsend, trecv, asend, arecv, bsend, brecv, gsend, grecv, dsend, drecv, psend, precv,
):
    CH = W // NZ
    i = lax.axis_index("stream")
    j = lax.axis_index("span")
    z = lax.rem(i, NZ)
    x = lax.div(i, NZ)

    def at_z(offset):
        return lax.rem(z + (offset + NZ), NZ)

    def line_z(zz):
        return (x * NZ + zz, j)

    span_left = (i, lax.rem(j + NS - 1, NS))
    span_right = (i, lax.rem(j + 1, NS))

    barrier = pltpu.get_barrier_semaphore()
    greeted = [line_z(at_z(d)) for d in range(1, NZ)] + [span_left, span_right]
    greeted += [(lax.rem(x + e, NX) * NZ + z, j) for e in range(1, NX)]
    for device in greeted:
        pl.semaphore_signal(barrier, inc=1, device_id=device, device_id_type=MESH)

    pairs = (
        (order_hbm, order_ref), (count_hbm, count_ref), (nbr_hbm, nbr_ref), (fid_hbm, fid_ref),
        (inv_hbm, inv_ref), (coup_hbm, coup_ref), (liftt_hbm, liftt_ref), (trop_hbm, trop_ref),
        (rhs_hbm, rhs_ref),
    )
    loads = [pltpu.make_async_copy(src, dst, insem.at[n]) for n, (src, dst) in enumerate(pairs)]
    for load in loads:
        load.start()

    tmap[:, :, :, TF:W, :] = jnp.zeros((2, NZ, 2, W - TF, 2 * W), BF16)
    tmap[:, :, :, W + TF :, :] = jnp.zeros((2, NZ, 2, W - TF, 2 * W), BF16)
    for ref in (prod, dmap):
        ref[...] = jnp.zeros(ref.shape, BF16)
    ltpad[...] = jnp.zeros(ltpad.shape, BF16)
    tpad[...] = jnp.zeros(tpad.shape, BF16)
    row = lax.broadcasted_iota(jnp.int32, (B, B), 0)
    col = lax.broadcasted_iota(jnp.int32, (B, B), 1)
    identity = jnp.where(row == col, 1.0, 0.0).astype(BF16)
    for load in loads:
        load.wait()

    a = order_ref[0, 0, 0]
    b = order_ref[0, 0, 1]
    a_is_0 = a == 0
    live = count_ref[0, 0] > 1
    zero_block = jnp.zeros((B, B), BF16)
    invs[0] = inv_ref[a]
    invs[1] = jnp.where(live, inv_ref[b], zero_block)
    for q in range(4):
        ltpad[q, 0:TF, :] = liftt_ref[q]
        lpad[q] = nt(identity, ltpad[q]).astype(BF16)
    for d in range(2):
        tpad[d, 0:TF, :] = trop_ref[1 - d]
    for pos, slot in ((0, a), (1, b)):
        for m in range(2):
            present = nbr_ref[0, 0, slot, m] < 2
            coups[pos, m] = jnp.where(present, coup_ref[fid_ref[0, 0, slot, m]], zero_block)
        base[pos] = rhs_ref[slot]

    def coupled(pos, v):
        high, low = split(v)
        v2 = jnp.concatenate([high, low], axis=1)
        both = jnp.dot(coups[pos, 0], v2, preferred_element_type=F32) + jnp.dot(
            coups[pos, 1], v2, preferred_element_type=F32
        )
        return both[:, :W] + both[:, W:]

    lane = lax.broadcasted_iota(jnp.int32, (TF, W), 1)

    def own_map(d):
        first, second = (0, 1) if d == 0 else (1, 0)
        u1 = jnp.dot(invs[first], lpad[d], preferred_element_type=F32)
        u2 = jnp.dot(invs[second], lpad[d], preferred_element_type=F32)
        v = apply(invs[second], coupled(second, u1))
        trace = trop_ref[1 - d]
        t11 = -apply(trace, u1)
        t22 = -apply(trace, u2)
        t21 = apply(trace, v)
        first_is_0 = jnp.where(a_is_0, 1.0 - d, 0.0 + d).astype(F32)
        flag = jnp.zeros((TF, W), F32) + first_is_0
        upper = jnp.where(lane < TF, t11, jnp.where(lane < 112, pltpu.roll(t22, 32, 1), flag))
        lower = jnp.where(lane < TF, t21, pltpu.roll(t22, TF, 1))
        tmsg[d, z, 0:TF, :] = upper
        tmsg[d, z, TF : 2 * TF, :] = lower

    def unpack(d, zz):
        p = zz if d == 0 else NZ - 1 - zz
        upper = tmsg[d, zz, 0:TF, :]
        lower = tmsg[d, zz, TF : 2 * TF, :]
        flag = jnp.sum(jnp.where(lane == 120, upper, 0.0), axis=1, keepdims=True) > 0.5
        zero = jnp.zeros((TF, W), F32)
        t11 = jnp.where(lane < TF, upper, zero)
        t21 = jnp.where(lane < TF, lower, zero)
        t22 = jnp.where(
            lane < 48,
            pltpu.roll(lower, 48, 1),
            jnp.where(lane < TF, pltpu.roll(upper, 96, 1), zero),
        )
        blocks = (
            (0, 0, jnp.where(flag, t11, t22)),
            (0, W, jnp.where(flag, zero, t21)),
            (W, 0, jnp.where(flag, t21, zero)),
            (W, W, jnp.where(flag, t22, t11)),
        )
        for row, col, block in blocks:
            high, low = split(block)
            tmap[d, p, 0, row : row + TF, col : col + W] = high
            tmap[d, p, 1, row : row + TF, col : col + W] = low

    reach = (NZ // 2, NZ - 1 - NZ // 2)

    def t_copy(d, ring, k, zz):
        step = 1 if ring == 0 else -1
        return pltpu.make_async_remote_copy(
            src_ref=tmsg.at[d, zz],
            dst_ref=tmsg.at[d, zz],
            send_sem=tsend.at[d, ring, k],
            recv_sem=trecv.at[d, ring, k],
            device_id=line_z(at_z(step)),
            device_id_type=MESH,
        )

    def t_begin(d):
        for ring in range(2):
            if reach[ring] > 0:
                t_copy(d, ring, 0, z).start()

    def t_step(d, k):
        for ring in range(2):
            if k > reach[ring]:
                continue
            source = at_z(-k if ring == 0 else k)
            t_copy(d, ring, k - 1, source).wait_recv()
            if k < reach[ring]:
                t_copy(d, ring, k, source).start()
        for ring in range(2):
            if k <= reach[ring]:
                unpack(d, at_z(-k if ring == 0 else k))

    def t_end(d):
        for ring in range(2):
            for k in range(reach[ring]):
                t_copy(d, ring, k, at_z(-k if ring == 0 else k)).wait_send()

    def multiply(left, right):
        high = jnp.concatenate([left[0, 0:TF, :], left[0, W : W + TF, :]], axis=0)
        low = jnp.concatenate([left[1, 0:TF, :], left[1, W : W + TF, :]], axis=0)
        return (
            jnp.dot(high, right[0], preferred_element_type=F32)
            + jnp.dot(high, right[1], preferred_element_type=F32)
            + jnp.dot(low, right[0], preferred_element_type=F32)
        )

    def keep(ref, value):
        for part, v in enumerate(split(value)):
            ref[part, 0:TF, :] = v[0:TF]
            ref[part, W : W + TF, :] = v[TF:]

    lane_d = lax.broadcasted_iota(jnp.int32, (2 * TF, W), 1)
    lane_q = lax.broadcasted_iota(jnp.int32, (TF // 2, W), 1)

    def d_copy(d, e, device):
        return pltpu.make_async_remote_copy(
            src_ref=dmsg.at[d],
            dst_ref=dbuf.at[d, e],
            send_sem=dsend.at[d, e],
            recv_sem=drecv.at[d, e],
            device_id=device,
            device_id_type=MESH,
        )

    def group_line(d, e):
        return ((x + e if d == 0 else x - e) * NZ + z, j)

    def group_map(d):
        xp = x if d == 0 else NX - 1 - x
        level = [tmap.at[d, p] for p in range(NZ)]
        slot = 0
        while len(level) > 2:
            joined = []
            for n in range(0, len(level), 2):
                keep(prod.at[slot], multiply(level[n + 1], level[n]))
                joined.append(prod.at[slot])
                slot += 1
            level = joined
        total = multiply(level[1], level[0])
        rolled = pltpu.roll(total[:, W:], TF, 1)
        dmsg[d, 0 : 2 * TF, :] = jnp.where(lane_d < TF, total[:, :W], rolled)
        quarter = TF // 2
        rest = rolled[0:quarter]
        for q in range(1, 4):
            rest = jnp.where(
                lane_q < 32 * q, rest, pltpu.roll(rolled[q * quarter : (q + 1) * quarter], 32 * q, 1)
            )
        dmsg[d, 2 * TF :, :] = rest
        for e in range(1, NX - 1):

            @pl.when(jnp.logical_and(xp >= 1, xp + e <= NX - 1))
            def _():
                d_copy(d, e, group_line(d, e)).start()

    def group_arrive(d):
        xp = x if d == 0 else NX - 1 - x
        for source in range(1, NX - 1):

            @pl.when(xp > source)
            def _():
                e = xp - source
                d_copy(d, e, group_line(d, -e)).wait_recv()
                main = dbuf[d, e, 0 : 2 * TF, :]
                rest = dbuf[d, e, 2 * TF :, :]
                spread = jnp.concatenate(
                    [rest] + [pltpu.roll(rest, W - 32 * q, 1) for q in range(1, 4)], axis=0
                )
                zero = jnp.zeros((2 * TF, W), F32)
                left = jnp.where(lane_d < TF, main, zero)
                rolled = jnp.where(lane_d >= TF, main, jnp.where(lane_d < 32, spread, zero))
                right = pltpu.roll(rolled, 48, 1)
                keep(dmap.at[d, source], jnp.concatenate([left, right], axis=1))

    def group_end(d):
        xp = x if d == 0 else NX - 1 - x
        for e in range(1, NX - 1):

            @pl.when(jnp.logical_and(xp >= 1, xp + e <= NX - 1))
            def _():
                d_copy(d, e, group_line(d, e)).wait_send()

    far_first = sorted(range(1, NZ), key=lambda d: (-min(d, NZ - d), d))

    def a_copy(h, d):
        zz = at_z(d)
        return pltpu.make_async_remote_copy(
            src_ref=sstage.at[h, pl.ds(pl.multiple_of(zz * CH, CH), CH), :],
            dst_ref=sbuf.at[h, z],
            send_sem=asend.at[h, d],
            recv_sem=arecv.at[h, d],
            device_id=line_z(zz),
            device_id_type=MESH,
        )

    def b_copy(h, d, p):
        return pltpu.make_async_remote_copy(
            src_ref=ostage.at[h, p],
            dst_ref=wbuf.at[h, pl.ds(pl.multiple_of(z * CH, CH), CH), :],
            send_sem=bsend.at[h, d],
            recv_sem=brecv.at[h, d],
            device_id=line_z(at_z(d)),
            device_id_type=MESH,
        )

    def g_copy(h, e, device):
        return pltpu.make_async_remote_copy(
            src_ref=gstage.at[h],
            dst_ref=gbuf.at[h, e],
            send_sem=gsend.at[h, e],
            recv_sem=grecv.at[h, e],
            device_id=device,
            device_id_type=MESH,
        )

    def p_copy(h, side, device):
        return pltpu.make_async_remote_copy(
            src_ref=pstage.at[h, side],
            dst_ref=pbuf.at[h, side],
            send_sem=psend.at[h, side],
            recv_sem=precv.at[h, side],
            device_id=device,
            device_id_type=MESH,
        )

    def solve(h, d, initial):
        first, second = (0, 1) if d == 0 else (1, 0)
        if initial:
            r1, r2 = base[first], base[second]
        else:
            r1, r2 = resid[first] - coupled(first, field[second]), resid[second]
        x1 = apply(invs[first], r1)
        x2 = apply(invs[second], r2 - coupled(second, x1))
        field[first] = x1
        field[second] = x2
        s1 = apply(tpad[d], x1)
        s2 = apply(tpad[d], x2)
        sa, sb = (s1, s2) if d == 0 else (s2, s1)
        sstage[h, :, 0:W] = jnp.where(a_is_0, sa, sb).T
        sstage[h, :, W : 2 * W] = jnp.where(a_is_0, sb, sa).T
        for dist in far_first:
            a_copy(h, dist).start()
        sbuf[h, z] = sstage[h, pl.ds(pl.multiple_of(z * CH, CH), CH), :]

    def at_start(k, d, action):
        if d == 0:
            pl.when(k == 0)(action)

    def finish(k, d):
        h = 2 * k + d
        first, second = (0, 1) if d == 0 else (1, 0)
        xp = x if d == 0 else NX - 1 - x
        for dist in far_first:
            a_copy(h, dist).wait_recv()

        def line_sum(p):
            return sbuf[h, p if d == 0 else NZ - 1 - p]

        v = line_sum(0)
        for p in range(1, NZ):
            v = through(v, tmap[d, p, 0], tmap[d, p, 1]) + line_sum(p)
        gstage[h] = v
        for e in range(1, NX):

            @pl.when(xp + e <= NX - 1)
            def _():
                g_copy(h, e, group_line(d, e)).start()

        def forward_group():
            group_map(0)
            t_step(1, 1)

        at_start(k, d, forward_group)
        pl.when(k == 0)(lambda: group_arrive(d))
        icur[...] = jnp.zeros((CH, 2 * W), F32)
        for source in range(NX - 1):

            @pl.when(xp > source)
            def _():
                e = xp - source
                g_copy(h, e, group_line(d, -e)).wait_recv()
                if source == 0:
                    icur[...] = gbuf[h, e]
                else:
                    icur[...] = gbuf[h, e] + through(
                        icur[...], dmap[d, source, 0], dmap[d, source, 1]
                    )

        v = icur[...]
        for p in range(NZ):
            ostage[h, p] = v
            if p < NZ - 1:
                v = through(v, tmap[d, p, 0], tmap[d, p, 1]) + line_sum(p)
        for dist in far_first:
            zz = at_z(dist)
            b_copy(h, dist, zz if d == 0 else NZ - 1 - zz).start()
        own = z if d == 0 else NZ - 1 - z
        wbuf[h, pl.ds(pl.multiple_of(z * CH, CH), CH), :] = ostage[h, own]

        def more_maps():
            for n in range(2, NZ // 2):
                t_step(1, n)

        at_start(k, d, more_maps)
        for dist in far_first:
            b_copy(h, dist, 0).wait_recv()

        w0 = wbuf[h, :, 0:W].T
        w1 = wbuf[h, :, W : 2 * W].T
        wa = jnp.where(a_is_0, w0, w1)
        wb = jnp.where(a_is_0, w1, w0)
        lifted = (apply(lpad[d], wa), apply(lpad[d], wb))
        y1 = apply(invs[first], lifted[first])
        y2 = apply(invs[second], lifted[second] - coupled(second, y1))
        x1 = field[first] - y1
        x2 = field[second] - y2
        field[first] = x1
        field[second] = x2

        def exchange():
            xa, xb = (x1, x2) if d == 0 else (x2, x1)
            for side, trace, device in ((0, 3, span_right), (1, 2, span_left)):
                ta = apply(trop_ref[trace], xa)
                tb = apply(trop_ref[trace], xb)
                pstage[h, side, 0] = jnp.where(a_is_0, ta, tb)
                pstage[h, side, 1] = jnp.where(a_is_0, tb, ta)
                p_copy(h, side, device).start()
            for pos in range(2):
                resid[pos] = base[pos] - lifted[pos]

            def last_maps():
                if NZ // 2 > 1:
                    t_step(1, NZ // 2)
                t_end(1)
                group_end(0)

            at_start(k, d, last_maps)
            p_copy(h, 0, span_right).wait_recv()
            p_copy(h, 1, span_left).wait_recv()
            for pos in range(2):
                total = resid[pos]
                for side in range(2):
                    t0 = pbuf[h, side, 0]
                    t1 = pbuf[h, side, 1]
                    mine, other = (t0, t1) if pos == 0 else (t1, t0)
                    total = total - apply(
                        lpad[2 + side, :, 0:TF], jnp.where(a_is_0, mine, other)
                    )
                resid[pos] = total
            p_copy(h, 0, span_right).wait_send()
            p_copy(h, 1, span_left).wait_send()

        if d == 0:
            exchange()
        else:
            pl.when(k < SWEEPS - 1)(exchange)

        for dist in far_first:
            a_copy(h, dist).wait_send()
            b_copy(h, dist, 0).wait_send()
        for e in range(1, NX):

            @pl.when(xp + e <= NX - 1)
            def _():
                g_copy(h, e, group_line(d, e)).wait_send()

    own_map(0)
    pl.semaphore_wait(barrier, len(greeted))
    t_begin(0)
    solve(0, 0, True)
    own_map(1)
    unpack(0, z)
    unpack(1, z)
    for k in range(1, NZ // 2 + 1):
        t_step(0, k)
    t_begin(1)
    t_end(0)

    def sweep(k, carry):
        finish(k, 0)
        solve(2 * k + 1, 1, False)

        @pl.when(k == 0)
        def _():
            group_map(1)

        finish(k, 1)

        @pl.when(k < SWEEPS - 1)
        def _():
            solve(2 * k + 2, 0, False)

        return carry

    lax.fori_loop(0, SWEEPS, sweep, 0)
    group_end(1)
    out_ref[0] = jnp.where(a_is_0, field[0], field[1])
    out_ref[1] = jnp.where(a_is_0, field[1], field[0])


def solution(mesh):
    lines = mesh.shape["stream"]
    NZ = {32: 8, 8: 4, 4: 2}[lines]
    NX = lines // NZ
    NS = mesh.shape["span"]
    CH = W // NZ
    H = 2 * SWEEPS

    def local(rhs, inv_blocks, coupling, trace_ops, lift_ops, order, counts, neighbours, face_ids):
        dma = pltpu.SemaphoreType.DMA
        call = pl.pallas_call(
            functools.partial(kernel, NX, NZ, NS),
            out_shape=jax.ShapeDtypeStruct((2, B, W), F32),
            in_specs=[pl.BlockSpec(memory_space=pl.ANY)] * 9,
            out_specs=pl.BlockSpec(memory_space=pltpu.VMEM),
            scratch_shapes=[
                pltpu.SMEM((1, 1, 2), jnp.int32),
                pltpu.SMEM((1, 1), jnp.int32),
                pltpu.SMEM((1, 1, 2, 2), jnp.int32),
                pltpu.SMEM((1, 1, 2, 2), jnp.int32),
                pltpu.VMEM((2, B, W), F32),
                pltpu.VMEM((2, B, B), BF16),
                pltpu.VMEM((6, B, B), BF16),
                pltpu.VMEM((4, TF, B), BF16),
                pltpu.VMEM((4, TF, B), BF16),
                pltpu.VMEM((2, B, B), BF16),
                pltpu.VMEM((2, 2, B, B), BF16),
                pltpu.VMEM((4, B, W), BF16),
                pltpu.VMEM((4, W, B), BF16),
                pltpu.VMEM((2, W, B), BF16),
                pltpu.VMEM((2, B, W), F32),
                pltpu.VMEM((2, B, W), F32),
                pltpu.VMEM((2, B, W), F32),
                pltpu.VMEM((2, NZ, 2 * TF, W), F32),
                pltpu.VMEM((2, NZ, 2, 2 * W, 2 * W), BF16),
                pltpu.VMEM((NZ, 2, 2 * W, 2 * W), BF16),
                pltpu.VMEM((2, NX, 2, 2 * W, 2 * W), BF16),
                pltpu.VMEM((2, 5 * TF // 2, W), F32),
                pltpu.VMEM((2, NX, 5 * TF // 2, W), F32),
                pltpu.VMEM((H, W, 2 * W), F32),
                pltpu.VMEM((H, NZ, CH, 2 * W), F32),
                pltpu.VMEM((H, NZ, CH, 2 * W), F32),
                pltpu.VMEM((H, W, 2 * W), F32),
                pltpu.VMEM((H, CH, 2 * W), F32),
                pltpu.VMEM((H, NX, CH, 2 * W), F32),
                pltpu.VMEM((CH, 2 * W), F32),
                pltpu.VMEM((H, 2, 2, TF, W), F32),
                pltpu.VMEM((H, 2, 2, TF, W), F32),
                dma((9,)),
                dma((2, 2, NZ)), dma((2, 2, NZ)),
                dma((H, NZ)), dma((H, NZ)),
                dma((H, NZ)), dma((H, NZ)),
                dma((H, NX)), dma((H, NX)),
                dma((2, NX)), dma((2, NX)),
                dma((H, 2)), dma((H, 2)),
            ],
            compiler_params=pltpu.CompilerParams(
                collective_id=0, has_side_effects=True, vmem_limit_bytes=60 << 20
            ),
        )
        result = call(
            order, counts, neighbours, face_ids,
            rhs[0, 0], inv_blocks[0, 0], coupling, trace_ops, lift_ops.transpose(0, 2, 1),
        )
        return result[None, None]

    placed = (
        P("stream", "span", None, None, None),
        P("stream", "span", None, None, None),
        P(),
        P(),
        P(),
        P("stream", "span", None),
        P("stream", "span"),
        P("stream", "span", None, None),
        P("stream", "span", None, None),
    )
    return jax.shard_map(
        local,
        mesh=mesh,
        in_specs=placed,
        out_specs=P("stream", "span", None, None, None),
        check_vma=False,
    )
```

time: 148 us -> 120 us (0.81)
  the two profiles are of different devices: /device:TPU:48 before, /device:TPU:32 now
where the time goes in v2:
time: 120 us
  Pallas kernels  117 us (98%)
  local copies, waits for them, and re-layouts  1.72 us (1%)
    pallas_call x1, Pallas kernels, local(): call(order, counts, neighbours, face_ids, rhs[0, 0], inv_blocks[0, 0], co...  117 us

profile of v2, /device:TPU:32, one launch (start us, length us, event | category | flops | bytes accessed | tf_op | source)
XLA Modules:
  0.0 119.9 jit_solution(4587014629980655004)
XLA Ops:
  0.7 117.5 %shard_map.91 = f32[2,320,128]{2,1,0:T(8,128)} custom-call(s32[1,1,2]{2,1,0:T(1,128)} %order_hbm.1, s32[1,1]{1,0:T(1,128)S(6)} %copy.11.count_hbm, s32[1,1,2,2]{3,2,1,0:T(2,128)} %nbr_hbm.1, s32[1,1,2,2]{3,2,1,0:T(2,128)} %fid_hbm.1, f32[2,320,128]{2,1,0:T(8,128)} %bitcast.6, bf16[2,320,320]{2,1,0:T(8,128)(2,1)} %bitcast.5, bf16[6,320,320]{2,1,0:T(8,128)(2,1)} %coup_hbm.1, ...), custom_call_target="tpu_custom_call" | custom-call | tf_op jit(solution)/shard_map/pallas_call | solution.py:557
  118.1 1.7 %copy.12 = f32[1,1,2,320,128]{4,3,2,1,0:T(8,128)} copy(f32[1,1,2,320,128]{4,3,2,1,0:T(8,128)} %bitcast.4) | data formatting | bytes 655360

commit v3 on v2

--- a/solution.py
+++ b/solution.py
@@ -44,6 +44,7 @@
     out_ref,
     order_ref, count_ref, nbr_ref, fid_ref, rhs_ref, inv_ref, coup_ref, trop_ref, liftt_ref,
     invs, coups, lpad, ltpad, tpad, base, resid, field,
+    kept, wmap, nmap, tloc, tfull, spar,
     tmsg, tmap, prod, dmap, dmsg, dbuf, sstage, sbuf, ostage, wbuf, gstage, gbuf, icur, pstage, pbuf,
     insem, tsend, trecv, asend, arecv, bsend, brecv, gsend, grecv, dsend, drecv, psend, precv,
 ):
@@ -79,7 +80,8 @@
 
     tmap[:, :, :, TF:W, :] = jnp.zeros((2, NZ, 2, W - TF, 2 * W), BF16)
     tmap[:, :, :, W + TF :, :] = jnp.zeros((2, NZ, 2, W - TF, 2 * W), BF16)
-    for ref in (prod, dmap):
+    tfull[...] = jnp.zeros(tfull.shape, F32)
+    for ref in (prod, dmap, wmap, nmap):
         ref[...] = jnp.zeros(ref.shape, BF16)
     ltpad[...] = jnp.zeros(ltpad.shape, BF16)
     tpad[...] = jnp.zeros(tpad.shape, BF16)
@@ -117,11 +119,17 @@
 
     lane = lax.broadcasted_iota(jnp.int32, (TF, W), 1)
 
+    def response(d, q):
+        first, second = (0, 1) if d == 0 else (1, 0)
+        u1 = jnp.dot(invs[first], lpad[q], preferred_element_type=F32)
+        u2 = jnp.dot(invs[second], lpad[q], preferred_element_type=F32)
+        v = apply(invs[second], coupled(second, u1))
+        return u1, u2, v
+
     def own_map(d):
-        first, second = (0, 1) if d == 0 else (1, 0)
-        u1 = jnp.dot(invs[first], lpad[d], preferred_element_type=F32)
-        u2 = jnp.dot(invs[second], lpad[d], preferred_element_type=F32)
-        v = apply(invs[second], coupled(second, u1))
+        u1, u2, v = response(d, d)
+        for n, part in enumerate((u1, u2, v)):
+            kept[d, n] = part
         trace = trop_ref[1 - d]
         t11 = -apply(trace, u1)
         t22 = -apply(trace, u2)
@@ -132,6 +140,35 @@
         lower = jnp.where(lane < TF, t21, pltpu.roll(t22, TF, 1))
         tmsg[d, z, 0:TF, :] = upper
         tmsg[d, z, TF : 2 * TF, :] = lower
+
+    def put(ref, row, col, value):
+        for part, v in enumerate(split(value)):
+            ref[part, row : row + value.shape[0], col : col + W] = v
+
+    def mapped(ref, v):
+        high, low = split(v)
+        both = jnp.concatenate([high, low], axis=1)
+        y = jnp.dot(ref[0], both, preferred_element_type=F32)
+        y = y[:, :W] + y[:, W:]
+        return y + jnp.dot(ref[1], high, preferred_element_type=F32)
+
+    def span_map(d):
+        first, second = (0, 1) if d == 0 else (1, 0)
+        for side, face in ((0, 3), (1, 2)):
+            trace = trop_ref[face]
+            rows = (2 * side + first) * TF, (2 * side + second) * TF
+            put(wmap.at[d], rows[0], first * W, apply(trace, kept[d, 0]))
+            put(wmap.at[d], rows[1], second * W, apply(trace, kept[d, 1]))
+            put(wmap.at[d], rows[1], first * W, -apply(trace, kept[d, 2]))
+
+    def entry_map(d):
+        first, second = (0, 1) if d == 0 else (1, 0)
+        for side in range(2):
+            u1, u2, v = response(d, 2 + side)
+            col = 2 * side * W
+            put(nmap.at[d], first * W, col + first * W, -apply(tpad[d], u1))
+            put(nmap.at[d], second * W, col + second * W, -apply(tpad[d], u2))
+            put(nmap.at[d], second * W, col + first * W, apply(tpad[d], v))
 
     def unpack(d, zz):
         p = zz if d == 0 else NZ - 1 - zz
@@ -159,30 +196,33 @@
 
     reach = (NZ // 2, NZ - 1 - NZ // 2)
 
-    def t_copy(d, ring, k, zz):
+    def t_copy(d, ring, k, zz, half):
         step = 1 if ring == 0 else -1
+        rows = pl.ds(half * TF, TF)
         return pltpu.make_async_remote_copy(
-            src_ref=tmsg.at[d, zz],
-            dst_ref=tmsg.at[d, zz],
-            send_sem=tsend.at[d, ring, k],
-            recv_sem=trecv.at[d, ring, k],
+            src_ref=tmsg.at[d, zz, rows, :],
+            dst_ref=tmsg.at[d, zz, rows, :],
+            send_sem=tsend.at[d, ring, k, half],
+            recv_sem=trecv.at[d, ring, k, half],
             device_id=line_z(at_z(step)),
             device_id_type=MESH,
         )
 
     def t_begin(d):
-        for ring in range(2):
-            if reach[ring] > 0:
-                t_copy(d, ring, 0, z).start()
+        for half in range(2):
+            for ring in range(2):
+                if reach[ring] > 0:
+                    t_copy(d, ring, 0, z, half).start()
 
     def t_step(d, k):
-        for ring in range(2):
-            if k > reach[ring]:
-                continue
-            source = at_z(-k if ring == 0 else k)
-            t_copy(d, ring, k - 1, source).wait_recv()
-            if k < reach[ring]:
-                t_copy(d, ring, k, source).start()
+        for half in range(2):
+            for ring in range(2):
+                if k > reach[ring]:
+                    continue
+                source = at_z(-k if ring == 0 else k)
+                t_copy(d, ring, k - 1, source, half).wait_recv()
+                if k < reach[ring]:
+                    t_copy(d, ring, k, source, half).start()
         for ring in range(2):
             if k <= reach[ring]:
                 unpack(d, at_z(-k if ring == 0 else k))
@@ -190,7 +230,8 @@
     def t_end(d):
         for ring in range(2):
             for k in range(reach[ring]):
-                t_copy(d, ring, k, at_z(-k if ring == 0 else k)).wait_send()
+                for half in range(2):
+                    t_copy(d, ring, k, at_z(-k if ring == 0 else k), half).wait_send()
 
     def multiply(left, right):
         high = jnp.concatenate([left[0, 0:TF, :], left[0, W : W + TF, :]], axis=0)
@@ -319,7 +360,7 @@
             device_id_type=MESH,
         )
 
-    def solve(h, d, initial):
+    def solve(d, initial):
         first, second = (0, 1) if d == 0 else (1, 0)
         if initial:
             r1, r2 = base[first], base[second]
@@ -329,14 +370,22 @@
         x2 = apply(invs[second], r2 - coupled(second, x1))
         field[first] = x1
         field[second] = x2
-        s1 = apply(tpad[d], x1)
-        s2 = apply(tpad[d], x2)
-        sa, sb = (s1, s2) if d == 0 else (s2, s1)
+        spar[first * W : first * W + W, :] = apply(tpad[d], x1)
+        spar[second * W : second * W + W, :] = apply(tpad[d], x2)
+
+    def send_line_traces(h, s):
+        sa, sb = s[0:W], s[W:]
         sstage[h, :, 0:W] = jnp.where(a_is_0, sa, sb).T
         sstage[h, :, W : 2 * W] = jnp.where(a_is_0, sb, sa).T
         for dist in far_first:
             a_copy(h, dist).start()
         sbuf[h, z] = sstage[h, pl.ds(pl.multiple_of(z * CH, CH), CH), :]
+
+    def local_span_traces():
+        for side, face in ((0, 3), (1, 2)):
+            for pos in range(2):
+                row = (2 * side + pos) * TF
+                tloc[row : row + TF, :] = apply(trop_ref[face], field[pos])
 
     def at_start(k, d, action):
         if d == 0:
@@ -396,6 +445,7 @@
         def more_maps():
             for n in range(2, NZ // 2):
                 t_step(1, n)
+            entry_map(0)
 
         at_start(k, d, more_maps)
         for dist in far_first:
@@ -405,24 +455,21 @@
         w1 = wbuf[h, :, W : 2 * W].T
         wa = jnp.where(a_is_0, w0, w1)
         wb = jnp.where(a_is_0, w1, w0)
-        lifted = (apply(lpad[d], wa), apply(lpad[d], wb))
-        y1 = apply(invs[first], lifted[first])
-        y2 = apply(invs[second], lifted[second] - coupled(second, y1))
-        x1 = field[first] - y1
-        x2 = field[second] - y2
-        field[first] = x1
-        field[second] = x2
-
-        def exchange():
-            xa, xb = (x1, x2) if d == 0 else (x2, x1)
-            for side, trace, device in ((0, 3, span_right), (1, 2, span_left)):
-                ta = apply(trop_ref[trace], xa)
-                tb = apply(trop_ref[trace], xb)
+        sides = ((0, span_right), (1, span_left))
+
+        def send_span_traces():
+            t = tloc[...] - mapped(wmap.at[d], jnp.concatenate([wa, wb], axis=0))
+            for side, device in sides:
+                ta = t[2 * side * TF : (2 * side + 1) * TF]
+                tb = t[(2 * side + 1) * TF : (2 * side + 2) * TF]
                 pstage[h, side, 0] = jnp.where(a_is_0, ta, tb)
                 pstage[h, side, 1] = jnp.where(a_is_0, tb, ta)
                 p_copy(h, side, device).start()
+
+        def prepare_next():
             for pos in range(2):
                 resid[pos] = base[pos] - lifted[pos]
+            solve(1 - d, False)
 
             def last_maps():
                 if NZ // 2 > 1:
@@ -431,25 +478,41 @@
                 group_end(0)
 
             at_start(k, d, last_maps)
-            p_copy(h, 0, span_right).wait_recv()
-            p_copy(h, 1, span_left).wait_recv()
-            for pos in range(2):
-                total = resid[pos]
-                for side in range(2):
-                    t0 = pbuf[h, side, 0]
-                    t1 = pbuf[h, side, 1]
-                    mine, other = (t0, t1) if pos == 0 else (t1, t0)
-                    total = total - apply(
-                        lpad[2 + side, :, 0:TF], jnp.where(a_is_0, mine, other)
-                    )
-                resid[pos] = total
-            p_copy(h, 0, span_right).wait_send()
-            p_copy(h, 1, span_left).wait_send()
-
-        if d == 0:
-            exchange()
+            for side, device in sides:
+                p_copy(h, side, device).wait_recv()
+                t0 = pbuf[h, side, 0]
+                t1 = pbuf[h, side, 1]
+                row = 2 * side * W
+                tfull[row : row + TF, :] = jnp.where(a_is_0, t0, t1)
+                tfull[row + W : row + W + TF, :] = jnp.where(a_is_0, t1, t0)
+            send_line_traces(h + 1, spar[...] + mapped(nmap.at[1 - d], tfull[...]))
+            taken = [
+                apply(lpad[2], tfull[pos * W : pos * W + W, :])
+                + apply(lpad[3], tfull[(2 + pos) * W : (2 + pos) * W + W, :])
+                for pos in range(2)
+            ]
+            z1 = apply(invs[second], taken[second])
+            z2 = apply(invs[first], taken[first] - coupled(first, z1))
+            field[second] = field[second] - z1
+            field[first] = field[first] - z2
+            local_span_traces()
+            for side, device in sides:
+                p_copy(h, side, device).wait_send()
+
+        more = d == 0
+        if more:
+            send_span_traces()
         else:
-            pl.when(k < SWEEPS - 1)(exchange)
+            pl.when(k < SWEEPS - 1)(send_span_traces)
+        lifted = (apply(lpad[d], wa), apply(lpad[d], wb))
+        y1 = apply(invs[first], lifted[first])
+        y2 = apply(invs[second], lifted[second] - coupled(second, y1))
+        field[first] = field[first] - y1
+        field[second] = field[second] - y2
+        if more:
+            prepare_next()
+        else:
+            pl.when(k < SWEEPS - 1)(prepare_next)
 
         for dist in far_first:
             a_copy(h, dist).wait_send()
@@ -463,29 +526,31 @@
     own_map(0)
     pl.semaphore_wait(barrier, len(greeted))
     t_begin(0)
-    solve(0, 0, True)
+    solve(0, True)
+    send_line_traces(0, spar[...])
     own_map(1)
     unpack(0, z)
-    unpack(1, z)
+    chunks = [
+        lambda: (span_map(0), unpack(1, z), local_span_traces()),
+        lambda: entry_map(1),
+        lambda: span_map(1),
+    ]
     for k in range(1, NZ // 2 + 1):
         t_step(0, k)
+        for chunk in chunks[:1] if k < NZ // 2 else chunks:
+            chunk()
+        chunks = chunks[1:]
     t_begin(1)
     t_end(0)
 
     def sweep(k, carry):
         finish(k, 0)
-        solve(2 * k + 1, 1, False)
 
         @pl.when(k == 0)
         def _():
             group_map(1)
 
         finish(k, 1)
-
-        @pl.when(k < SWEEPS - 1)
-        def _():
-            solve(2 * k + 2, 0, False)
-
         return carry
 
     lax.fori_loop(0, SWEEPS, sweep, 0)
@@ -527,6 +592,12 @@
                 pltpu.VMEM((2, B, W), F32),
                 pltpu.VMEM((2, B, W), F32),
                 pltpu.VMEM((2, B, W), F32),
+                pltpu.VMEM((2, 3, B, W), F32),
+                pltpu.VMEM((2, 2, 4 * TF, 2 * W), BF16),
+                pltpu.VMEM((2, 2, 2 * W, 4 * W), BF16),
+                pltpu.VMEM((4 * TF, W), F32),
+                pltpu.VMEM((4 * W, W), F32),
+                pltpu.VMEM((2 * W, W), F32),
                 pltpu.VMEM((2, NZ, 2 * TF, W), F32),
                 pltpu.VMEM((2, NZ, 2, 2 * W, 2 * W), BF16),
                 pltpu.VMEM((NZ, 2, 2 * W, 2 * W), BF16),
@@ -543,7 +614,7 @@
                 pltpu.VMEM((H, 2, 2, TF, W), F32),
                 pltpu.VMEM((H, 2, 2, TF, W), F32),
                 dma((9,)),
-                dma((2, 2, NZ)), dma((2, 2, NZ)),
+                dma((2, 2, NZ, 2)), dma((2, 2, NZ, 2)),
                 dma((H, NZ)), dma((H, NZ)),
                 dma((H, NZ)), dma((H, NZ)),
                 dma((H, NX)), dma((H, NX)),

time: 120 us -> 115 us (0.958)
  the two profiles are of different devices: /device:TPU:32 before, /device:TPU:24 now
where the time goes in v3:
time: 115 us
  Pallas kernels  113 us (98%)
  local copies, waits for them, and re-layouts  1.72 us (1%)
    pallas_call x1, Pallas kernels, local(): call(order, counts, neighbours, face_ids, rhs[0, 0], inv_blocks[0, 0], co...  113 us

profile of v3, /device:TPU:24, one launch (start us, length us, event | category | flops | bytes accessed | tf_op | source)
XLA Modules:
  0.0 115.2 jit_solution(12189866531482756708)
XLA Ops:
  0.7 112.8 %shard_map.91 = f32[2,320,128]{2,1,0:T(8,128)} custom-call(s32[1,1,2]{2,1,0:T(1,128)} %order_hbm.1, s32[1,1]{1,0:T(1,128)S(6)} %copy.11.count_hbm, s32[1,1,2,2]{3,2,1,0:T(2,128)} %nbr_hbm.1, s32[1,1,2,2]{3,2,1,0:T(2,128)} %fid_hbm.1, f32[2,320,128]{2,1,0:T(8,128)} %bitcast.6, bf16[2,320,320]{2,1,0:T(8,128)(2,1)} %bitcast.5, bf16[6,320,320]{2,1,0:T(8,128)(2,1)} %coup_hbm.1, ...), custom_call_target="tpu_custom_call" | custom-call | tf_op jit(solution)/shard_map/pallas_call | solution.py:628
  113.4 1.7 %copy.12 = f32[1,1,2,320,128]{4,3,2,1,0:T(8,128)} copy(f32[1,1,2,320,128]{4,3,2,1,0:T(8,128)} %bitcast.4) | data formatting | bytes 655360

commit v4 on v3

--- a/solution.py
+++ b/solution.py
@@ -45,7 +45,7 @@
     order_ref, count_ref, nbr_ref, fid_ref, rhs_ref, inv_ref, coup_ref, trop_ref, liftt_ref,
     invs, coups, lpad, ltpad, tpad, base, resid, field,
     kept, wmap, nmap, tloc, tfull, spar,
-    tmsg, tmap, prod, dmap, dmsg, dbuf, sstage, sbuf, ostage, wbuf, gstage, gbuf, icur, pstage, pbuf,
+    tmsg, tmap, prod, dmap, dmsg, dbuf, sstage, sbuf, lsum, ostage, wbuf, gstage, gbuf, icur, pstage, pbuf,
     insem, tsend, trecv, asend, arecv, bsend, brecv, gsend, grecv, dsend, drecv, psend, precv,
 ):
     CH = W // NZ
@@ -81,14 +81,19 @@
     tmap[:, :, :, TF:W, :] = jnp.zeros((2, NZ, 2, W - TF, 2 * W), BF16)
     tmap[:, :, :, W + TF :, :] = jnp.zeros((2, NZ, 2, W - TF, 2 * W), BF16)
     tfull[...] = jnp.zeros(tfull.shape, F32)
-    for ref in (prod, dmap, wmap, nmap):
+    for ref in (wmap, nmap):
         ref[...] = jnp.zeros(ref.shape, BF16)
+    gap = W - TF
+    for d in range(2):
+        for rows in (pl.ds(TF, gap), pl.ds(W + TF, gap)):
+            prod[d, :, :, rows, :] = jnp.zeros((prod.shape[1], 2, gap, 2 * W), BF16)
+            dmap[d, :, :, rows, :] = jnp.zeros((dmap.shape[1], 2, gap, 2 * W), BF16)
     ltpad[...] = jnp.zeros(ltpad.shape, BF16)
     tpad[...] = jnp.zeros(tpad.shape, BF16)
     row = lax.broadcasted_iota(jnp.int32, (B, B), 0)
     col = lax.broadcasted_iota(jnp.int32, (B, B), 1)
     identity = jnp.where(row == col, 1.0, 0.0).astype(BF16)
-    for load in loads:
+    for load in loads[:-1]:
         load.wait()
 
     a = order_ref[0, 0, 0]
@@ -98,16 +103,15 @@
     zero_block = jnp.zeros((B, B), BF16)
     invs[0] = inv_ref[a]
     invs[1] = jnp.where(live, inv_ref[b], zero_block)
-    for q in range(4):
+
+    def take_lift(q):
         ltpad[q, 0:TF, :] = liftt_ref[q]
         lpad[q] = nt(identity, ltpad[q]).astype(BF16)
-    for d in range(2):
-        tpad[d, 0:TF, :] = trop_ref[1 - d]
-    for pos, slot in ((0, a), (1, b)):
+
+    def take_coupling(pos, slot):
         for m in range(2):
             present = nbr_ref[0, 0, slot, m] < 2
             coups[pos, m] = jnp.where(present, coup_ref[fid_ref[0, 0, slot, m]], zero_block)
-        base[pos] = rhs_ref[slot]
 
     def coupled(pos, v):
         high, low = split(v)
@@ -263,18 +267,22 @@
     def group_line(d, e):
         return ((x + e if d == 0 else x - e) * NZ + z, j)
 
+    def map_levels(d):
+        levels = [[tmap.at[d, p] for p in range(NZ)]]
+        slot = 0
+        while len(levels[-1]) > 2:
+            count = len(levels[-1]) // 2
+            levels.append([prod.at[d, slot + n] for n in range(count)])
+            slot += count
+        return levels
+
     def group_map(d):
         xp = x if d == 0 else NX - 1 - x
-        level = [tmap.at[d, p] for p in range(NZ)]
-        slot = 0
-        while len(level) > 2:
-            joined = []
-            for n in range(0, len(level), 2):
-                keep(prod.at[slot], multiply(level[n + 1], level[n]))
-                joined.append(prod.at[slot])
-                slot += 1
-            level = joined
-        total = multiply(level[1], level[0])
+        levels = map_levels(d)
+        for lower, upper in zip(levels, levels[1:]):
+            for n, ref in enumerate(upper):
+                keep(ref, multiply(lower[2 * n + 1], lower[2 * n]))
+        total = multiply(levels[-1][1], levels[-1][0])
         rolled = pltpu.roll(total[:, W:], TF, 1)
         dmsg[d, 0 : 2 * TF, :] = jnp.where(lane_d < TF, total[:, :W], rolled)
         quarter = TF // 2
@@ -307,7 +315,7 @@
                 left = jnp.where(lane_d < TF, main, zero)
                 rolled = jnp.where(lane_d >= TF, main, jnp.where(lane_d < 32, spread, zero))
                 right = pltpu.roll(rolled, 48, 1)
-                keep(dmap.at[d, source], jnp.concatenate([left, right], axis=1))
+                keep(dmap.at[d, source - 1], jnp.concatenate([left, right], axis=1))
 
     def group_end(d):
         xp = x if d == 0 else NX - 1 - x
@@ -319,10 +327,31 @@
 
     far_first = sorted(range(1, NZ), key=lambda d: (-min(d, NZ - d), d))
 
+    def lanes_of(v):
+        return lax.broadcasted_iota(jnp.int32, v.shape, 1)
+
+    def pack(v0, v1):
+        rolled = pltpu.roll(v1, TF, 1)
+        half = CH // 2
+        main = jnp.where(lanes_of(v0) < TF, v0, rolled)
+        upper = rolled[:half]
+        return main, jnp.where(lanes_of(upper) < 32, upper, pltpu.roll(rolled[half:], 32, 1))
+
+    def unpacked(main, rest):
+        lanes = lanes_of(main)
+        zero = jnp.zeros(main.shape, F32)
+        rolled = jnp.where(lanes >= TF, main, jnp.where(lanes < 32, rest, zero))
+        return jnp.where(lanes < TF, main, zero), pltpu.roll(rolled, 48, 1)
+
+    def unpack_piece(piece):
+        rest = piece[CH:]
+        rest = jnp.concatenate([rest, pltpu.roll(rest, 96, 1)], axis=0)
+        return jnp.concatenate(unpacked(piece[:CH], rest), axis=1)
+
     def a_copy(h, d):
         zz = at_z(d)
         return pltpu.make_async_remote_copy(
-            src_ref=sstage.at[h, pl.ds(pl.multiple_of(zz * CH, CH), CH), :],
+            src_ref=sstage.at[h, zz],
             dst_ref=sbuf.at[h, z],
             send_sem=asend.at[h, d],
             recv_sem=arecv.at[h, d],
@@ -333,7 +362,7 @@
     def b_copy(h, d, p):
         return pltpu.make_async_remote_copy(
             src_ref=ostage.at[h, p],
-            dst_ref=wbuf.at[h, pl.ds(pl.multiple_of(z * CH, CH), CH), :],
+            dst_ref=wbuf.at[h, z],
             send_sem=bsend.at[h, d],
             recv_sem=brecv.at[h, d],
             device_id=line_z(at_z(d)),
@@ -375,11 +404,16 @@
 
     def send_line_traces(h, s):
         sa, sb = s[0:W], s[W:]
-        sstage[h, :, 0:W] = jnp.where(a_is_0, sa, sb).T
-        sstage[h, :, W : 2 * W] = jnp.where(a_is_0, sb, sa).T
+        s0 = jnp.where(a_is_0, sa, sb).T
+        s1 = jnp.where(a_is_0, sb, sa).T
+        for zz in range(NZ):
+            rows = slice(zz * CH, (zz + 1) * CH)
+            main, rest = pack(s0[rows], s1[rows])
+            sstage[h, zz, 0:CH, :] = main
+            sstage[h, zz, CH:, :] = rest
         for dist in far_first:
             a_copy(h, dist).start()
-        sbuf[h, z] = sstage[h, pl.ds(pl.multiple_of(z * CH, CH), CH), :]
+        sbuf[h, z] = sstage[h, z]
 
     def local_span_traces():
         for side, face in ((0, 3), (1, 2)):
@@ -395,15 +429,22 @@
         h = 2 * k + d
         first, second = (0, 1) if d == 0 else (1, 0)
         xp = x if d == 0 else NX - 1 - x
+        at_start(k, d, lambda: group_map(0))
         for dist in far_first:
             a_copy(h, dist).wait_recv()
 
-        def line_sum(p):
-            return sbuf[h, p if d == 0 else NZ - 1 - p]
-
-        v = line_sum(0)
-        for p in range(1, NZ):
-            v = through(v, tmap[d, p, 0], tmap[d, p, 1]) + line_sum(p)
+        for zz in range(NZ):
+            p = zz if d == 0 else NZ - 1 - zz
+            lsum[p] = unpack_piece(sbuf[h, zz])
+        levels = map_levels(d)
+        sums = [[lsum[p] for p in range(NZ)]]
+        for maps in levels:
+            low = sums[-1]
+            sums.append([
+                through(low[n], maps[n + 1][0], maps[n + 1][1]) + low[n + 1]
+                for n in range(0, len(low), 2)
+            ])
+        v = sums[-1][0]
         gstage[h] = v
         for e in range(1, NX):
 
@@ -411,11 +452,7 @@
             def _():
                 g_copy(h, e, group_line(d, e)).start()
 
-        def forward_group():
-            group_map(0)
-            t_step(1, 1)
-
-        at_start(k, d, forward_group)
+        at_start(k, d, lambda: t_step(1, 1))
         pl.when(k == 0)(lambda: group_arrive(d))
         icur[...] = jnp.zeros((CH, 2 * W), F32)
         for source in range(NX - 1):
@@ -428,19 +465,23 @@
                     icur[...] = gbuf[h, e]
                 else:
                     icur[...] = gbuf[h, e] + through(
-                        icur[...], dmap[d, source, 0], dmap[d, source, 1]
+                        icur[...], dmap[d, source - 1, 0], dmap[d, source - 1, 1]
                     )
 
-        v = icur[...]
+        flows = [icur[...]]
+        for maps, low in zip(levels[::-1], sums[-2::-1]):
+            wider = []
+            for n, v in enumerate(flows):
+                wider += [v, through(v, maps[2 * n][0], maps[2 * n][1]) + low[2 * n]]
+            flows = wider
         for p in range(NZ):
-            ostage[h, p] = v
-            if p < NZ - 1:
-                v = through(v, tmap[d, p, 0], tmap[d, p, 1]) + line_sum(p)
+            for part, v in zip((pl.ds(0, CH), pl.ds(CH, CH // 2)), pack(flows[p][:, :W], flows[p][:, W:])):
+                ostage[h, p, part, :] = v
         for dist in far_first:
             zz = at_z(dist)
             b_copy(h, dist, zz if d == 0 else NZ - 1 - zz).start()
         own = z if d == 0 else NZ - 1 - z
-        wbuf[h, pl.ds(pl.multiple_of(z * CH, CH), CH), :] = ostage[h, own]
+        wbuf[h, z] = ostage[h, own]
 
         def more_maps():
             for n in range(2, NZ // 2):
@@ -451,8 +492,14 @@
         for dist in far_first:
             b_copy(h, dist, 0).wait_recv()
 
-        w0 = wbuf[h, :, 0:W].T
-        w1 = wbuf[h, :, W : 2 * W].T
+        main = jnp.concatenate([wbuf[h, zz, 0:CH, :] for zz in range(NZ)], axis=0)
+        rest = jnp.concatenate([wbuf[h, zz, CH:, :] for zz in range(NZ)], axis=0)
+        moved = pltpu.roll(rest, 96, 1)
+        half = CH // 2
+        rest = jnp.concatenate(
+            [r[zz * half : (zz + 1) * half] for zz in range(NZ) for r in (rest, moved)], axis=0
+        )
+        w0, w1 = (w.T for w in unpacked(main, rest))
         wa = jnp.where(a_is_0, w0, w1)
         wb = jnp.where(a_is_0, w1, w0)
         sides = ((0, span_right), (1, span_left))
@@ -523,16 +570,25 @@
             def _():
                 g_copy(h, e, group_line(d, e)).wait_send()
 
+    take_lift(0)
+    take_coupling(1, b)
     own_map(0)
     pl.semaphore_wait(barrier, len(greeted))
     t_begin(0)
+    for d in range(2):
+        tpad[d, 0:TF, :] = trop_ref[1 - d]
+    take_coupling(0, a)
+    loads[-1].wait()
+    base[0] = rhs_ref[a]
+    base[1] = rhs_ref[b]
     solve(0, True)
     send_line_traces(0, spar[...])
+    take_lift(1)
     own_map(1)
     unpack(0, z)
     chunks = [
         lambda: (span_map(0), unpack(1, z), local_span_traces()),
-        lambda: entry_map(1),
+        lambda: (take_lift(2), take_lift(3), entry_map(1)),
         lambda: span_map(1),
     ]
     for k in range(1, NZ // 2 + 1):
@@ -600,14 +656,15 @@
                 pltpu.VMEM((2 * W, W), F32),
                 pltpu.VMEM((2, NZ, 2 * TF, W), F32),
                 pltpu.VMEM((2, NZ, 2, 2 * W, 2 * W), BF16),
-                pltpu.VMEM((NZ, 2, 2 * W, 2 * W), BF16),
-                pltpu.VMEM((2, NX, 2, 2 * W, 2 * W), BF16),
+                pltpu.VMEM((2, max(NZ - 2, 1), 2, 2 * W, 2 * W), BF16),
+                pltpu.VMEM((2, max(NX - 2, 1), 2, 2 * W, 2 * W), BF16),
                 pltpu.VMEM((2, 5 * TF // 2, W), F32),
                 pltpu.VMEM((2, NX, 5 * TF // 2, W), F32),
-                pltpu.VMEM((H, W, 2 * W), F32),
-                pltpu.VMEM((H, NZ, CH, 2 * W), F32),
-                pltpu.VMEM((H, NZ, CH, 2 * W), F32),
-                pltpu.VMEM((H, W, 2 * W), F32),
+                pltpu.VMEM((H, NZ, 3 * CH // 2, W), F32),
+                pltpu.VMEM((H, NZ, 3 * CH // 2, W), F32),
+                pltpu.VMEM((NZ, CH, 2 * W), F32),
+                pltpu.VMEM((H, NZ, 3 * CH // 2, W), F32),
+                pltpu.VMEM((H, NZ, 3 * CH // 2, W), F32),
                 pltpu.VMEM((H, CH, 2 * W), F32),
                 pltpu.VMEM((H, NX, CH, 2 * W), F32),
                 pltpu.VMEM((CH, 2 * W), F32),

time: 115 us -> 108 us (0.939)
  Pallas kernels: 113 us -> 106 us
    pallas_call x1, Pallas kernels: 113 us -> 106 us  [local(): call(order, counts, neighbours, face_ids, rhs[0, 0], inv_blocks[0, 0], co...]
where the time goes in v4:
time: 108 us
  Pallas kernels  106 us (98%)
  local copies, waits for them, and re-layouts  1.72 us (2%)
    pallas_call x1, Pallas kernels, local(): call(order, counts, neighbours, face_ids, rhs[0, 0], inv_blocks[0, 0], co...  106 us

profile of v4, /device:TPU:24, one launch (start us, length us, event | category | flops | bytes accessed | tf_op | source)
XLA Modules:
  0.0 108.0 jit_solution(16416294679215912821)
XLA Ops:
  0.7 105.6 %shard_map.91 = f32[2,320,128]{2,1,0:T(8,128)} custom-call(s32[1,1,2]{2,1,0:T(1,128)} %order_hbm.1, s32[1,1]{1,0:T(1,128)S(6)} %copy.11.count_hbm, s32[1,1,2,2]{3,2,1,0:T(2,128)} %nbr_hbm.1, s32[1,1,2,2]{3,2,1,0:T(2,128)} %fid_hbm.1, f32[2,320,128]{2,1,0:T(8,128)} %bitcast.6, bf16[2,320,320]{2,1,0:T(8,128)(2,1)} %bitcast.5, bf16[6,320,320]{2,1,0:T(8,128)(2,1)} %coup_hbm.1, ...), custom_call_target="tpu_custom_call" | custom-call | tf_op jit(solution)/shard_map/pallas_call | solution.py:685
  106.2 1.7 %copy.12 = f32[1,1,2,320,128]{4,3,2,1,0:T(8,128)} copy(f32[1,1,2,320,128]{4,3,2,1,0:T(8,128)} %bitcast.4) | data formatting | bytes 655360

commit v5 on v4

--- a/solution.py
+++ b/solution.py
@@ -44,7 +44,7 @@
     out_ref,
     order_ref, count_ref, nbr_ref, fid_ref, rhs_ref, inv_ref, coup_ref, trop_ref, liftt_ref,
     invs, coups, lpad, ltpad, tpad, base, resid, field,
-    kept, wmap, nmap, tloc, tfull, spar,
+    kept, rmap, wmap, nmap, tloc, tfull, spar,
     tmsg, tmap, prod, dmap, dmsg, dbuf, sstage, sbuf, lsum, ostage, wbuf, gstage, gbuf, icur, pstage, pbuf,
     insem, tsend, trecv, asend, arecv, bsend, brecv, gsend, grecv, dsend, drecv, psend, precv,
 ):
@@ -158,6 +158,10 @@
 
     def span_map(d):
         first, second = (0, 1) if d == 0 else (1, 0)
+        put(rmap.at[d], first * B, first * W, kept[d, 0])
+        put(rmap.at[d], first * B, second * W, jnp.zeros((B, W), F32))
+        put(rmap.at[d], second * B, second * W, kept[d, 1])
+        put(rmap.at[d], second * B, first * W, -kept[d, 2])
         for side, face in ((0, 3), (1, 2)):
             trace = trop_ref[face]
             rows = (2 * side + first) * TF, (2 * side + second) * TF
@@ -503,9 +507,10 @@
         wa = jnp.where(a_is_0, w0, w1)
         wb = jnp.where(a_is_0, w1, w0)
         sides = ((0, span_right), (1, span_left))
+        inflow = jnp.concatenate([wa, wb], axis=0)
 
         def send_span_traces():
-            t = tloc[...] - mapped(wmap.at[d], jnp.concatenate([wa, wb], axis=0))
+            t = tloc[...] - mapped(wmap.at[d], inflow)
             for side, device in sides:
                 ta = t[2 * side * TF : (2 * side + 1) * TF]
                 tb = t[(2 * side + 1) * TF : (2 * side + 2) * TF]
@@ -514,8 +519,8 @@
                 p_copy(h, side, device).start()
 
         def prepare_next():
-            for pos in range(2):
-                resid[pos] = base[pos] - lifted[pos]
+            resid[0] = base[0] - apply(lpad[d], wa)
+            resid[1] = base[1] - apply(lpad[d], wb)
             solve(1 - d, False)
 
             def last_maps():
@@ -551,11 +556,9 @@
             send_span_traces()
         else:
             pl.when(k < SWEEPS - 1)(send_span_traces)
-        lifted = (apply(lpad[d], wa), apply(lpad[d], wb))
-        y1 = apply(invs[first], lifted[first])
-        y2 = apply(invs[second], lifted[second] - coupled(second, y1))
-        field[first] = field[first] - y1
-        field[second] = field[second] - y2
+        taken = mapped(rmap.at[d], inflow)
+        field[0] = field[0] - taken[0:B]
+        field[1] = field[1] - taken[B:]
         if more:
             prepare_next()
         else:
@@ -582,7 +585,6 @@
     base[0] = rhs_ref[a]
     base[1] = rhs_ref[b]
     solve(0, True)
-    send_line_traces(0, spar[...])
     take_lift(1)
     own_map(1)
     unpack(0, z)
@@ -593,6 +595,8 @@
     ]
     for k in range(1, NZ // 2 + 1):
         t_step(0, k)
+        if k == max(NZ // 2 - 2, 1):
+            send_line_traces(0, spar[...])
         for chunk in chunks[:1] if k < NZ // 2 else chunks:
             chunk()
         chunks = chunks[1:]
@@ -627,7 +631,7 @@
         dma = pltpu.SemaphoreType.DMA
         call = pl.pallas_call(
             functools.partial(kernel, NX, NZ, NS),
-            out_shape=jax.ShapeDtypeStruct((2, B, W), F32),
+            out_shape=pltpu.VMEM((2, B, W), F32),
             in_specs=[pl.BlockSpec(memory_space=pl.ANY)] * 9,
             out_specs=pl.BlockSpec(memory_space=pltpu.VMEM),
             scratch_shapes=[
@@ -649,6 +653,7 @@
                 pltpu.VMEM((2, B, W), F32),
                 pltpu.VMEM((2, B, W), F32),
                 pltpu.VMEM((2, 3, B, W), F32),
+                pltpu.VMEM((2, 2, 2 * B, 2 * W), BF16),
                 pltpu.VMEM((2, 2, 4 * TF, 2 * W), BF16),
                 pltpu.VMEM((2, 2, 2 * W, 4 * W), BF16),
                 pltpu.VMEM((4 * TF, W), F32),

time: 108 us -> 103 us (0.954)
  the two profiles are of different devices: /device:TPU:24 before, /device:TPU:32 now
where the time goes in v5:
time: 103 us
  Pallas kernels  102 us (99%)
    pallas_call x1, Pallas kernels, local(): call(order, counts, neighbours, face_ids, rhs[0, 0], inv_blocks[0, 0], co...  102 us

profile of v5, /device:TPU:32, one launch (start us, length us, event | category | flops | bytes accessed | tf_op | source)
XLA Modules:
  0.0 103.2 jit_solution(743177259073941155)
XLA Ops:
  0.7 101.9 %shard_map.91 = f32[2,320,128]{2,1,0:T(8,128)S(1)} custom-call(s32[1,1,2]{2,1,0:T(1,128)} %order_hbm.1, s32[1,1]{1,0:T(1,128)S(6)} %copy.12.count_hbm, s32[1,1,2,2]{3,2,1,0:T(2,128)} %nbr_hbm.1, s32[1,1,2,2]{3,2,1,0:T(2,128)} %fid_hbm.1, f32[2,320,128]{2,1,0:T(8,128)} %bitcast.6, bf16[2,320,320]{2,1,0:T(8,128)(2,1)} %bitcast.5, ...), custom_call_target="tpu_custom_call" | custom-call | tf_op jit(solution)/shard_map/pallas_call | solution.py:690
  102.5 0.7 copy.11

commit v6 on v5

--- a/solution.py
+++ b/solution.py
@@ -204,33 +204,33 @@
 
     reach = (NZ // 2, NZ - 1 - NZ // 2)
 
-    def t_copy(d, ring, k, zz, half):
+    def t_copy(d, ring, k, zz, quarter):
         step = 1 if ring == 0 else -1
-        rows = pl.ds(half * TF, TF)
+        rows = pl.ds(quarter * (TF // 2), TF // 2)
         return pltpu.make_async_remote_copy(
             src_ref=tmsg.at[d, zz, rows, :],
             dst_ref=tmsg.at[d, zz, rows, :],
-            send_sem=tsend.at[d, ring, k, half],
-            recv_sem=trecv.at[d, ring, k, half],
+            send_sem=tsend.at[d, ring, k, quarter],
+            recv_sem=trecv.at[d, ring, k, quarter],
             device_id=line_z(at_z(step)),
             device_id_type=MESH,
         )
 
     def t_begin(d):
-        for half in range(2):
+        for quarter in range(4):
             for ring in range(2):
                 if reach[ring] > 0:
-                    t_copy(d, ring, 0, z, half).start()
+                    t_copy(d, ring, 0, z, quarter).start()
 
     def t_step(d, k):
-        for half in range(2):
+        for quarter in range(4):
             for ring in range(2):
                 if k > reach[ring]:
                     continue
                 source = at_z(-k if ring == 0 else k)
-                t_copy(d, ring, k - 1, source, half).wait_recv()
+                t_copy(d, ring, k - 1, source, quarter).wait_recv()
                 if k < reach[ring]:
-                    t_copy(d, ring, k, source, half).start()
+                    t_copy(d, ring, k, source, quarter).start()
         for ring in range(2):
             if k <= reach[ring]:
                 unpack(d, at_z(-k if ring == 0 else k))
@@ -238,8 +238,8 @@
     def t_end(d):
         for ring in range(2):
             for k in range(reach[ring]):
-                for half in range(2):
-                    t_copy(d, ring, k, at_z(-k if ring == 0 else k), half).wait_send()
+                for quarter in range(4):
+                    t_copy(d, ring, k, at_z(-k if ring == 0 else k), quarter).wait_send()
 
     def multiply(left, right):
         high = jnp.concatenate([left[0, 0:TF, :], left[0, W : W + TF, :]], axis=0)
@@ -676,7 +676,7 @@
                 pltpu.VMEM((H, 2, 2, TF, W), F32),
                 pltpu.VMEM((H, 2, 2, TF, W), F32),
                 dma((9,)),
-                dma((2, 2, NZ, 2)), dma((2, 2, NZ, 2)),
+                dma((2, 2, NZ, 4)), dma((2, 2, NZ, 4)),
                 dma((H, NZ)), dma((H, NZ)),
                 dma((H, NZ)), dma((H, NZ)),
                 dma((H, NX)), dma((H, NX)),

time: 103 us -> 104 us (level)
  no operation moved by 1% of the time
where the time goes in v6:
time: 104 us
  Pallas kernels  102 us (98%)
    pallas_call x1, Pallas kernels, local(): call(order, counts, neighbours, face_ids, rhs[0, 0], inv_blocks[0, 0], co...  102 us

profile of v6, /device:TPU:32, one launch (start us, length us, event | category | flops | bytes accessed | tf_op | source)
XLA Modules:
  0.0 103.6 jit_solution(11835230886602415620)
XLA Ops:
  0.7 102.3 %shard_map.91 = f32[2,320,128]{2,1,0:T(8,128)S(1)} custom-call(s32[1,1,2]{2,1,0:T(1,128)} %order_hbm.1, s32[1,1]{1,0:T(1,128)S(6)} %copy.12.count_hbm, s32[1,1,2,2]{3,2,1,0:T(2,128)} %nbr_hbm.1, s32[1,1,2,2]{3,2,1,0:T(2,128)} %fid_hbm.1, f32[2,320,128]{2,1,0:T(8,128)} %bitcast.6, bf16[2,320,320]{2,1,0:T(8,128)(2,1)} %bitcast.5, ...), custom_call_target="tpu_custom_call" | custom-call | tf_op jit(solution)/shard_map/pallas_call | solution.py:690
  102.9 0.7 copy.11
